TPU v7x, 32 devices: a whole 2x2x4 slice. The times are simulated.
32 devices in a mesh: rows: 16 (over z, x, core), mlp: 2 (over y).
Axes of the slice: x: 2, y: 2, z: 4, core: 2. Of those that a mesh axis runs over, the one named last changes fastest.
Arguments:
- node_rows: bfloat16 [16384, 512], P(('rows', 'mlp')), may hold values from -6 to 6
- noise_cond: bfloat16 [8, 128], replicated, may hold values from -6 to 6
- sample_id: int32 [16384], P(('rows', 'mlp')), may hold values from 0 to 7, as said below
- neighbours: int32 [16384, 16], P(('rows', 'mlp')), may hold values from 0 to 16383, as said below
- ada_weight: bfloat16 [128, 2048], replicated, may hold values from -0.25 to 0.25
- ada_bias: bfloat16 [2048], replicated, may hold values from -3 to 3
- query_weight: bfloat16 [512, 512], replicated, may hold values from -0.25 to 0.25
- keyval_weight: bfloat16 [512, 1024], replicated, may hold values from -0.25 to 0.25
- out_weight: bfloat16 [512, 512], replicated, may hold values from -0.5 to 0.5
- up_weight: bfloat16 [512, 2048], P(None, 'mlp'), may hold values from -0.25 to 0.25
- up_bias: bfloat16 [2048], P('mlp'), may hold values from -3 to 3
- down_weight: bfloat16 [2048, 512], P('mlp'), may hold values from -0.125 to 0.125
- down_bias: bfloat16 [512], replicated, may hold values from -3 to 3
- cotangent: bfloat16 [16384, 512], P(('rows', 'mlp')), may hold values from -6 to 6
Outputs:
- layer_out: bfloat16 [16384, 512], P(('rows', 'mlp'))
- grad_rows: float32 [16384, 512], P(('rows', 'mlp'))
- grad_cond: float32 [8, 128], replicated
- grad_ada_weight: float32 [128, 2048], replicated
- grad_ada_bias: float32 [2048], replicated
- grad_query_weight: float32 [512, 512], replicated
- grad_keyval_weight: float32 [512, 1024], replicated
- grad_out_weight: float32 [512, 512], replicated
- grad_up_weight: float32 [512, 2048], P(None, 'mlp')
- grad_up_bias: float32 [2048], P('mlp')
- grad_down_weight: float32 [2048, 512], P('mlp')
- grad_down_bias: float32 [512], replicated
Inputs may be any that keep to these rules, and one draw needn't show every extreme that they name: Row n stands for mesh node n // 8 of sample sample_id[n]. Each of its 16 neighbours is a row of the same sample whose node differs by at most 64, counted cyclically over the 2048 nodes; so it lies within 512 positions of n, counted cyclically over 16384. The first two are the rows of nodes one below and one above, cyclically. sample_id[n] depends only on n mod 8, and each sample is carried by 2048 rows.
All inputs are finite; a program needn't handle non-finite values.
Results may differ from a plain program's by a relative error of at most 0.012.
The roundings to bfloat16 on the way count: a program that leaves them out, or rounds other values in their place, can miss the bound.
Values may be sent and summed in bfloat16 or wider, within the bound.
A program may use at most 192 MiB of HBM per device.

v0:
```python
import math

import jax
import jax.numpy as jnp
from jax import lax
from jax.sharding import PartitionSpec as P

HEADS = 4


EPSILON = 1e-05
PRECISE = lax.Precision.HIGHEST


def with_halo(x, sides, width):
    for axis, dim in sides:
        peers, length = (lax.axis_size(axis), x.shape[dim])
        up = [(i, (i + 1) % peers) for i in range(peers)]
        down = [(j, i) for i, j in up]
        last = lax.slice_in_dim(x, length - width, length, axis=dim)
        leading = lax.slice_in_dim(x, 0, width, axis=dim)
        before = lax.ppermute(last, axis, up)
        after = lax.ppermute(leading, axis, down)
        x = jnp.concatenate([before, x, after], axis=dim)
    return x


def shifted(x, axis, by):
    peers = lax.axis_size(axis)
    return lax.ppermute(x, axis, [(i, (i + by) % peers) for i in range(peers)])


def layer_norm(values):
    centred = values - jnp.mean(values, axis=-1, keepdims=True)
    inverse = lax.rsqrt(jnp.mean(centred * centred, axis=-1, keepdims=True) + EPSILON)
    return (centred * inverse, inverse)


def norm_back(grad_norm, normed, inverse):
    return inverse * (
        grad_norm
        - jnp.mean(grad_norm, axis=-1, keepdims=True)
        - normed * jnp.mean(grad_norm * normed, axis=-1, keepdims=True)
    )


def bf_dot(left_operand, right_operand):
    return jnp.dot(left_operand, right_operand, preferred_element_type=jnp.float32)


def split_heads(picked, feature_width, head_count):
    row_total, near_count = (picked.shape[0], picked.shape[1])
    head_size = feature_width // head_count
    keys_near = picked[:, :, :feature_width].reshape(row_total, near_count, head_count, head_size)
    values_near = picked[:, :, feature_width:].reshape(row_total, near_count, head_count, head_size)
    return (keys_near, values_near)


def swish_back(grad_active, hidden):
    logistic = jax.nn.sigmoid(hidden)
    return (grad_active * logistic * (1.0 + hidden * (1.0 - logistic))).astype(jnp.bfloat16)


def shards(
    node_rows,
    noise_cond,
    sample_id,
    neighbours,
    ada_weight,
    ada_bias,
    query_weight,
    keyval_weight,
    out_weight,
    up_weight,
    up_bias,
    down_weight,
    down_bias,
    cotangent,
):
    row_count, feature_width = node_rows.shape
    head_count = HEADS
    head_size = feature_width // head_count
    near_count = neighbours.shape[1]
    factor = 1.0 / math.sqrt(head_size)
    samples = noise_cond.shape[0]
    devices = lax.axis_size(("rows", "mlp"))
    first_row = lax.axis_index(("rows", "mlp")) * row_count
    block_rows = min(row_count, 512)
    blocks = row_count // block_rows
    inputs = node_rows.astype(jnp.float32)
    modulation = bf_dot(noise_cond, ada_weight) + ada_bias.astype(jnp.float32)
    onehot = (sample_id[:, None] == jnp.arange(samples, dtype=jnp.int32)[None, :]).astype(
        jnp.float32
    )
    modrows = jnp.dot(onehot, modulation, precision=PRECISE)
    local_index = jnp.mod(neighbours - first_row + row_count, row_count * devices)
    index_blocks = local_index.reshape(blocks, block_rows, near_count)
    norm_one, inverse_one = layer_norm(inputs)
    normed_one = (
        norm_one * (1.0 + modrows[:, :feature_width])
        + modrows[:, feature_width : 2 * feature_width]
    ).astype(jnp.bfloat16)
    queries = bf_dot(normed_one, query_weight).astype(jnp.bfloat16)
    keyvals = bf_dot(normed_one, keyval_weight).astype(jnp.bfloat16)
    kv_table = with_halo(keyvals, ((("rows", "mlp"), 0),), row_count)

    def attend(block_items):
        query_part, index_part = block_items
        keys_near, values_near = split_heads(kv_table[index_part], feature_width, head_count)
        scores = (
            jnp.einsum("bhe,bjhe->bhj", query_part, keys_near, preferred_element_type=jnp.float32)
            * factor
        )
        highest = jnp.max(scores, axis=-1, keepdims=True)
        exponent = jnp.exp(scores - highest)
        denominator = jnp.sum(exponent, axis=-1, keepdims=True)
        attn_probs = (exponent / denominator).astype(jnp.bfloat16)
        mixture = jnp.einsum(
            "bhj,bjhe->bhe", attn_probs, values_near, preferred_element_type=jnp.float32
        )
        return (
            mixture.reshape(block_rows, feature_width).astype(jnp.bfloat16),
            (highest + jnp.log(denominator))[..., 0],
        )

    mixture, log_total = lax.map(
        attend, (queries.reshape(blocks, block_rows, head_count, head_size), index_blocks)
    )
    mixture = mixture.reshape(row_count, feature_width)
    middle = inputs + bf_dot(mixture, out_weight)
    norm_two, inverse_two = layer_norm(middle)
    normed_two = (
        norm_two * (1.0 + modrows[:, 2 * feature_width : 3 * feature_width])
        + modrows[:, 3 * feature_width :]
    ).astype(jnp.bfloat16)
    gathered = lax.all_gather(normed_two, "mlp", axis=0, tiled=True)
    hidden = bf_dot(gathered, up_weight) + up_bias.astype(jnp.float32)
    active = jax.nn.silu(hidden).astype(jnp.bfloat16)
    branch = lax.psum_scatter(bf_dot(active, down_weight), "mlp", scatter_dimension=0, tiled=True)
    layer_out = (middle + branch + down_bias.astype(jnp.float32)).astype(jnp.bfloat16)
    grad_out = cotangent.astype(jnp.float32)
    cot_rows = lax.all_gather(cotangent, "mlp", axis=0, tiled=True)
    grad_hidden = swish_back(bf_dot(cot_rows, down_weight.T), hidden)
    grad_two = lax.psum_scatter(
        bf_dot(grad_hidden, up_weight.T), "mlp", scatter_dimension=0, tiled=True
    )
    up_share = bf_dot(gathered.T, grad_hidden)
    upb_share = jnp.sum(grad_hidden.astype(jnp.float32), axis=0)
    down_share = bf_dot(active.T, cot_rows)
    grad_up, grad_upb, grad_down = lax.psum((up_share, upb_share, down_share), "rows")
    grad_middle = grad_out + norm_back(
        grad_two * (1.0 + modrows[:, 2 * feature_width : 3 * feature_width]), norm_two, inverse_two
    )
    grad_attended = grad_middle.astype(jnp.bfloat16)
    output_share = bf_dot(mixture.T, grad_attended)
    grad_mixture = bf_dot(grad_attended, out_weight.T).astype(jnp.bfloat16)
    queries_back = bf_dot(normed_one, query_weight).astype(jnp.bfloat16)
    table_back = with_halo(
        bf_dot(normed_one, keyval_weight).astype(jnp.bfloat16), ((("rows", "mlp"), 0),), row_count
    )

    def attend_back(table_grad, block_items):
        query_part, index_part, log_part, grad_part = block_items
        keys_near, values_near = split_heads(table_back[index_part], feature_width, head_count)
        scores = (
            jnp.einsum("bhe,bjhe->bhj", query_part, keys_near, preferred_element_type=jnp.float32)
            * factor
        )
        attn_exact = jnp.exp(scores - log_part[..., None])
        attn_probs = attn_exact.astype(jnp.bfloat16)
        grad_heads = grad_part.reshape(block_rows, head_count, head_size)
        grad_probs = jnp.einsum(
            "bhe,bjhe->bhj", grad_heads, values_near, preferred_element_type=jnp.float32
        )
        grad_scores = (
            attn_exact * (grad_probs - jnp.sum(attn_exact * grad_probs, axis=-1, keepdims=True))
        ).astype(jnp.bfloat16)
        grad_query = (
            jnp.einsum("bhj,bjhe->bhe", grad_scores, keys_near, preferred_element_type=jnp.float32)
            * factor
        )
        grad_keys = (
            jnp.einsum("bhj,bhe->bjhe", grad_scores, query_part, preferred_element_type=jnp.float32)
            * factor
        )
        grad_values = jnp.einsum(
            "bhj,bhe->bjhe", attn_probs, grad_heads, preferred_element_type=jnp.float32
        )
        grad_near = jnp.concatenate(
            [
                grad_keys.reshape(block_rows, near_count, feature_width),
                grad_values.reshape(block_rows, near_count, feature_width),
            ],
            axis=-1,
        )
        table_grad = table_grad.at[index_part.reshape(-1)].add(
            grad_near.reshape(block_rows * near_count, 2 * feature_width)
        )
        return (table_grad, grad_query.reshape(block_rows, feature_width).astype(jnp.bfloat16))

    table_grad, grad_queries = lax.scan(
        attend_back,
        jnp.zeros((3 * row_count, 2 * feature_width), jnp.float32),
        (
            queries_back.reshape(blocks, block_rows, head_count, head_size),
            index_blocks,
            log_total,
            grad_mixture.reshape(blocks, block_rows, feature_width),
        ),
    )
    grad_queries = grad_queries.reshape(row_count, feature_width)
    from_upper = shifted(table_grad[:row_count], ("rows", "mlp"), -1)
    from_lower = shifted(table_grad[2 * row_count :], ("rows", "mlp"), 1)
    grad_keyvals = (table_grad[row_count : 2 * row_count] + from_upper + from_lower).astype(
        jnp.bfloat16
    )
    query_share = bf_dot(normed_one.T, grad_queries)
    keyval_share = bf_dot(normed_one.T, grad_keyvals)
    grad_one = bf_dot(grad_queries, query_weight.T) + bf_dot(grad_keyvals, keyval_weight.T)
    grad_rows = grad_middle + norm_back(
        grad_one * (1.0 + modrows[:, :feature_width]), norm_one, inverse_one
    )
    grad_modrows = jnp.concatenate(
        [grad_one * norm_one, grad_one, grad_two * norm_two, grad_two], axis=1
    )
    modulation_share = jnp.dot(onehot.T, grad_modrows, precision=PRECISE)
    summed = lax.psum(
        (query_share, keyval_share, output_share, modulation_share, jnp.sum(grad_out, axis=0)),
        ("rows", "mlp"),
    )
    grad_query_weight, grad_keyval_weight, grad_out_weight, grad_modulation, grad_down_bias = summed
    grad_ada_weight = jnp.dot(noise_cond.astype(jnp.float32).T, grad_modulation, precision=PRECISE)
    grad_ada_bias = jnp.sum(grad_modulation, axis=0)
    grad_cond = jnp.dot(grad_modulation, ada_weight.astype(jnp.float32).T, precision=PRECISE)
    return (
        layer_out,
        grad_rows,
        grad_cond,
        grad_ada_weight,
        grad_ada_bias,
        grad_query_weight,
        grad_keyval_weight,
        grad_out_weight,
        grad_up,
        grad_upb,
        grad_down,
        grad_down_bias,
    )


def solution(mesh):
    placed = (
        P(("rows", "mlp"), None),
        P(),
        P(("rows", "mlp")),
        P(("rows", "mlp"), None),
        P(),
        P(),
        P(),
        P(),
        P(),
        P(None, "mlp"),
        P("mlp"),
        P("mlp", None),
        P(),
        P(("rows", "mlp"), None),
    )
    return jax.shard_map(
        shards,
        mesh=mesh,
        in_specs=placed,
        out_specs=(
            P(("rows", "mlp"), None),
            P(("rows", "mlp"), None),
            P(),
            P(),
            P(),
            P(),
            P(),
            P(),
            P(None, "mlp"),
            P("mlp"),
            P("mlp", None),
            P(),
        ),
        check_vma=False,
    )
```

profile of v0, /device:TPU:0, one launch (start us, length us, event | category | flops | bytes accessed | tf_op | source)
XLA Modules:
  0.0 817.1 jit_solution(563137369281137952)
XLA Ops:
  18.6 6.4 collective-permute-start.1
  26.3 30.0 %collective-permute-done.1 = bf16[512,1024]{1,0:T(8,128)(2,1)} collective-permute-done((bf16[512,1024]{1,0:T(8,128)(2,1)}, bf16[512,1024]{1,0:T(8,128)(2,1)}, u32[]{:S(2)}, u32[]{:S(2)}) %collective-permute-start.1) | collective-permute-done | bytes 1048608 | tf_op jit(solution)/shard_map/ppermute | solution.py:23
  57.2 3.2 pad_maximum_fusion
  60.4 42.8 %gather_fusion = bf16[8192,1024]{1,0:T(8,128)(2,1)} fusion(bf16[1536,1024]{1,0:T(8,128)(2,1)} %pad_maximum_fusion, s32[8192]{0:T(1024)S(1)} %broadcast_clamp_fusion), kind=kCustom, calls=%fused_computation | custom fusion | bytes 33587200 | tf_op jit(solution)/shard_map/while/body/eval_jaxpr/gather | solution.py:109
  103.2 18.5 %slice_bitcast_fusion.1 = (bf16[512,2,4,8,128]{4,3,2,1,0:T(8,128)(2,1)}, bf16[512,2,4,8,128]{4,3,2,1,0:T(8,128)(2,1)}, bf16[512,16,512]{2,1,0:T(8,128)(2,1)}, bf16[512,16,512]{2,1,0:T(8,128)(2,1)}) fusion(bf16[512,16,1024]{2,1,0:T(8,128)(2,1)} %bitcast.86), kind=kLoop, calls=%fused_computation.125 | loop fusion | bytes 50331648
  121.7 12.5 %reshape.162 = bf16[512,16,4,128]{3,2,1,0:T(4,128)(2,1)} reshape(bf16[512,16,512]{2,1,0:T(8,128)(2,1)} %get-tuple-element.104) | data formatting | bytes 16777216 | tf_op jit(solution)/shard_map/while/body/eval_jaxpr/reshape | solution.py:54
  134.2 12.9 %multiply_reduce_fusion.1 = f32[512,4,16]{1,2,0:T(8,128)} fusion(f32[512,4,128]{2,1,0:T(4,128)S(1)} %copy.76, bf16[512,16,4,128]{3,2,1,0:T(4,128)(2,1)} %reshape.162), kind=kLoop, calls=%fused_computation.10 | loop fusion | flops 12550144 | bytes 9568256
  151.0 5.7 fusion.8
  161.1 32.3 %all-gather.3.cloned.1.call-done = bf16[1024,512]{1,0:T(8,128)(2,1)} async-done(((bf16[512,512]{1,0:T(8,128)(2,1)}), bf16[1024,512]{1,0:T(8,128)(2,1)}) %all-gather.3.cloned.1.call-update) | async-done | bytes 1048592 | tf_op jit(solution)/shard_map/all_gather | solution.py:136
  193.4 5.5 multiply_convert_fusion.1
  198.9 17.4 %all-gather.5.cloned.1.call-done = bf16[1024,512]{1,0:T(8,128)(2,1)} async-done(((bf16[512,512]{1,0:T(8,128)(2,1)}), bf16[1024,512]{1,0:T(8,128)(2,1)}) %all-gather.5.cloned.1.call-update) | async-done | bytes 1048592 | tf_op jit(solution)/shard_map/all_gather | solution.py:142
  216.3 5.1 convert_reduce_fusion
  225.4 4.4 fusion.72
  230.6 3.5 copy.50
  234.1 12.6 %reshape.163 = bf16[512,16,4,128]{3,2,1,0:T(4,128)(2,1)} reshape(bf16[512,16,512]{2,1,0:T(8,128)(2,1)} %get-tuple-element.105) | data formatting | bytes 16777216 | tf_op jit(solution)/shard_map/while/body/eval_jaxpr/reshape | solution.py:55
  246.7 10.6 %reduce-scatter.5.cloned.1.call-done = f32[512,512]{1,0:T(8,128)} async-done(((f32[1024,512]{1,0:T(8,128)}), f32[512,512]{1,0:T(8,128)}) %reduce-scatter.5.cloned.1.call-update) | async-done | bytes 1048592 | tf_op jit(solution)/shard_map/reduce_scatter | solution.py:144
  259.3 32.6 %reduce-scatter.3.cloned.1.call-done = f32[512,512]{1,0:T(8,128)} async-done(((f32[1024,512]{1,0:T(8,128)}), f32[512,512]{1,0:T(8,128)}) %reduce-scatter.3.cloned.1.call-update) | async-done | bytes 1048592 | tf_op jit(solution)/shard_map/reduce_scatter | solution.py:139
  291.9 3.7 fusion.41
  299.2 24.5 %broadcast_multiply_fusion = (f32[512,4,128,16]{2,1,3,0:T(4,128)}, f32[512,4,16]{1,2,0:T(8,128)}) fusion(f32[512,4,128]{2,1,0:T(4,128)S(1)} %copy.77, f32[512,4,16]{1,2,0:T(8,128)} %copy.50, bf16[512,16,4,128]{3,2,1,0:T(4,128)(2,1)} %reshape.163), kind=kLoop, calls=%fused_computation.18 | loop fusion | flops 16744448 | bytes 26476544 | tf_op jit(solution)/shard_map/while/body/eval_jaxpr/bhj,bhe->bjhe/dot_general | solution.py:186
  323.7 12.7 %copy.114 = f32[1024,8,4,128]{3,1,2,0:T(8,128)} copy(f32[1024,8,4,128]{3,2,1,0:T(4,128)} %bitcast.88) | data formatting | bytes 33554432
  342.5 11.0 %multiply_multiply_fusion = f32[512,4,128,16]{2,1,3,0:T(4,128)S(1)} fusion(f32[512,4,128]{2,1,0:T(4,128)S(1)} %copy-done.7, f32[512,4,16]{1,2,0:T(8,128)} %copy.48), kind=kLoop, calls=%fused_computation.11 | loop fusion | flops 8388608 | bytes 17956864 | tf_op jit(solution)/shard_map/while/body/eval_jaxpr/mul | solution.py:183
  353.5 7.2 copy.115
  360.7 72.1 %scatter_custom_fusion = f32[1536,1024]{1,0:T(8,128)} fusion(s32[8192]{0:T(1024)S(1)} %bitcast.100, f32[8192,512]{1,0:T(8,128)} %bitcast.87, f32[]{:T(128)} %constant.96.clone.1, f32[8192,512]{1,0:T(8,128)} %bitcast.89, f32[]{:T(128)} %constant.55.clone.1), kind=kCustom, calls=%fused_computation.3 | custom fusion | flops 16777216 | bytes 39845896 | tf_op jit(solution)/shard_map/while/body/eval_jaxpr/scatter-add | solution.py:196
  432.8 4.8 fusion.70
  437.6 3.7 collective-permute-start.2
  442.0 5.8 fusion.5
  451.5 56.3 %collective-permute-done.2 = f32[512,1024]{1,0:T(8,128)} collective-permute-done((f32[512,1024]{1,0:T(8,128)}, f32[512,1024]{1,0:T(8,128)}, u32[]{:S(2)}, u32[]{:S(2)}) %collective-permute-start.2) | collective-permute-done | bytes 2097184 | tf_op jit(solution)/shard_map/ppermute | solution.py:30
  507.7 3.4 fusion.21
  523.6 57.0 %psum.61 = f32[1024]{0:T(1024)} all-reduce(f32[1024]{0:T(1024)S(1)} %get-tuple-element.123), channel_id=1, replica_groups=mesh['rows'=16,'mlp'=2] {'rows'}, use_global_device_ids=true, to_apply=%region_21.22 | all-reduce | flops 1024 | bytes 8192 | tf_op jit(solution)/shard_map/psum | solution.py:150
  580.5 37.2 %psum.63 = f32[512]{0:T(512)} all-reduce(f32[512]{0:T(512)S(1)} %get-tuple-element.115), channel_id=1, replica_groups=mesh['rows'=16,'mlp'=2] {'rows','mlp'}, use_global_device_ids=true, to_apply=%region_24.25 | all-reduce | flops 512 | bytes 4096 | tf_op jit(solution)/shard_map/psum | solution.py:227
  617.7 67.6 %all-reduce.5.cloned.1.call-done = (f32[8,2048]{1,0:T(8,128)}, f32[512,512]{1,0:T(8,128)}, f32[512,1024]{1,0:T(8,128)}, f32[512,512]{1,0:T(8,128)}) async-done(((f32[8,2048]{1,0:T(8,128)}, f32[512,512]{1,0:T(8,128)}, f32[512,1024]{1,0:T(8,128)}, f32[512,512]{1,0:T(8,128)}), (f32[8,2048]{1,0:T(8,128)}, f32[512,512]{1,0:T(8,128)}, f32[512,1024]{1,0:T(8,128)}, ...) | async-done | bytes 4259856 | tf_op jit(solution)/shard_map/psum | solution.py:227
  691.9 108.9 %all-reduce.7.cloned.1.call-done = (f32[512,1024]{1,0:T(8,128)}, f32[1024,512]{1,0:T(8,128)}) async-done(((f32[512,1024]{1,0:T(8,128)}, f32[1024,512]{1,0:T(8,128)}), (f32[512,1024]{1,0:T(8,128)}, f32[1024,512]{1,0:T(8,128)})) %all-reduce.7.cloned.1.call-update) | async-done | bytes 4194320 | tf_op jit(solution)/shard_map/psum | solution.py:150
  (148 shorter events, 70.4 us)
Async XLA Ops:
  7.2 186.2 %copy-start = (bf16[512,1024]{1,0:T(8,128)(2,1)S(1)}, bf16[512,1024]{1,0:T(8,128)(2,1)}, u32[]{:S(2)}) copy-start(bf16[512,1024]{1,0:T(8,128)(2,1)} %param.23) | copy-start | bytes 3145732
  7.2 9.4 %copy-start.5 = (bf16[512,512]{1,0:T(8,128)(2,1)S(1)}, bf16[512,512]{1,0:T(8,128)(2,1)}, u32[]{:S(2)}) copy-start(bf16[512,512]{1,0:T(8,128)(2,1)} %param.14) | copy-start | bytes 1572868
  7.2 186.2 %all-gather.3.cloned.1.call-start = ((), (), s32[]{:S(2)}) async-start(), calls=%async_computation.2 | async-start | bytes 1572864 | tf_op jit(solution)/shard_map/all_gather | solution.py:136
  8.6 8.3 %copy-start.24 = (f32[512]{0:T(512)}, f32[512]{0:T(512)S(1)}, u32[]{:S(2)}) copy-start(f32[512]{0:T(512)S(1)} %broadcast_multiply_fusion.6) | copy-start | bytes 6148
  8.6 8.3 %copy-start.21 = (bf16[512,1024]{1,0:T(8,128)(2,1)S(1)}, bf16[512,1024]{1,0:T(8,128)(2,1)}, u32[]{:S(2)}) copy-start(bf16[512,1024]{1,0:T(8,128)(2,1)} %param.21) | copy-start | bytes 3145732
  10.0 8.6 %copy-start.26 = (f32[512]{0:T(512)}, f32[512]{0:T(512)S(1)}, u32[]{:S(2)}) copy-start(f32[512]{0:T(512)S(1)} %add_rsqrt_fusion.1) | copy-start | bytes 6148
  12.0 13.2 %copy-start.28 = (s32[512,16]{0,1:T(8,128)S(1)}, s32[512,16]{0,1:T(8,128)}, u32[]{:S(2)}) copy-start(s32[512,16]{0,1:T(8,128)} %param.17) | copy-start | bytes 98308
  16.6 8.9 %copy-start.16 = (bf16[512,512]{1,0:T(8,128)(2,1)S(1)}, bf16[512,512]{1,0:T(8,128)(2,1)}, u32[]{:S(2)}) copy-start(bf16[512,512]{1,0:T(8,128)(2,1)} %param.20) | copy-start | bytes 1572868
  16.9 9.1 %copy-start.8 = (bf16[512,512]{1,0:T(8,128)(2,1)}, bf16[512,512]{1,0:T(8,128)(2,1)S(1)}, u32[]{:S(2)}) copy-start(bf16[512,512]{1,0:T(8,128)(2,1)S(1)} %fusion.32) | copy-start | bytes 1572868
  18.6 37.7 %collective-permute-start.1 = (bf16[512,1024]{1,0:T(8,128)(2,1)}, bf16[512,1024]{1,0:T(8,128)(2,1)}, u32[]{:S(2)}, u32[]{:S(2)}) collective-permute-start(bf16[512,1024]{1,0:T(8,128)(2,1)} %convolution_convert_fusion), channel_id=1, source_target_pairs={{1,0},{2,1},{3,2},{4,3},{5,4},{6,5},{7,6},{8,7},{9,8},{10,9},{11,1... | collective-permute-start | bytes 3145736 | tf_op jit(solution)/shard_map/ppermute | solution.py:23
  25.0 32.2 %collective-permute-start = (bf16[512,1024]{1,0:T(8,128)(2,1)}, bf16[512,1024]{1,0:T(8,128)(2,1)}, u32[]{:S(2)}, u32[]{:S(2)}) collective-permute-start(bf16[512,1024]{1,0:T(8,128)(2,1)} %convolution_convert_fusion), channel_id=1, source_target_pairs={{0,1},{1,2},{2,3},{3,4},{4,5},{5,6},{6,7},{7,8},{8,9},{9,10},{10,1... | collective-permute-start | bytes 3145736 | tf_op jit(solution)/shard_map/ppermute | solution.py:22
  26.3 107.9 %copy-start.6 = (f32[512,4,128]{2,1,0:T(4,128)}, f32[512,4,128]{2,1,0:T(4,128)S(1)}, u32[]{:S(2)}) copy-start(f32[512,4,128]{2,1,0:T(4,128)S(1)} %copy.76) | copy-start | bytes 3145732
  151.0 6.0 copy-start.18
  160.1 56.2 %all-gather.5.cloned.1.call-start = ((), (), s32[]{:S(2)}) async-start(), calls=%async_computation.4 | async-start | bytes 1572864 | tf_op jit(solution)/shard_map/all_gather | solution.py:142
  160.8 96.5 %reduce-scatter.5.cloned.1.call-start = ((), (), s32[]{:S(2)}) async-start(), calls=%async_computation.5 | async-start | bytes 3145728 | tf_op jit(solution)/shard_map/reduce_scatter | solution.py:144
  225.3 66.6 %reduce-scatter.3.cloned.1.call-start = ((), (), s32[]{:S(2)}) async-start(), calls=%async_computation.3 | async-start | bytes 3145728 | tf_op jit(solution)/shard_map/reduce_scatter | solution.py:139
  225.3 4.9 copy-start.32
  229.8 455.5 %all-reduce.5.cloned.1.call-start = ((), (), s32[]{:S(2)}) async-start(), calls=%async_computation.6 | async-start | bytes 8519680 | tf_op jit(solution)/shard_map/psum | solution.py:227
  336.3 6.1 copy-start.7
  437.6 70.2 %collective-permute-start.2 = (f32[512,1024]{1,0:T(8,128)}, f32[512,1024]{1,0:T(8,128)}, u32[]{:S(2)}, u32[]{:S(2)}) collective-permute-start(f32[512,1024]{1,0:T(8,128)} %get-tuple-element.106), channel_id=1, source_target_pairs={{0,31},{1,0},{2,1},{3,2},{4,3},{5,4},{6,5},{7,6},{8,7},{9,8},{10,9... | collective-permute-start | bytes 6291464 | tf_op jit(solution)/shard_map/ppermute | solution.py:30
  441.2 66.5 %collective-permute-start.3 = (f32[512,1024]{1,0:T(8,128)}, f32[512,1024]{1,0:T(8,128)}, u32[]{:S(2)}, u32[]{:S(2)}) collective-permute-start(f32[512,1024]{1,0:T(8,128)} %get-tuple-element.107), channel_id=1, source_target_pairs={{0,1},{1,2},{2,3},{3,4},{4,5},{5,6},{6,7},{7,8},{8,9},{9,10},{10,1... | collective-permute-start | bytes 6291464 | tf_op jit(solution)/shard_map/ppermute | solution.py:30
  442.0 6.1 copy-start.9
  442.0 7.5 copy-start.17
  451.4 61.8 %copy-start.4 = (f32[512,2048]{1,0:T(8,128)S(1)}, f32[512,2048]{1,0:T(8,128)}, u32[]{:S(2)}) copy-start(f32[512,2048]{1,0:T(8,128)} %copy-done.2) | copy-start | bytes 12582916
  451.4 61.8 %copy-start.22 = (bf16[512,1024]{1,0:T(8,128)(2,1)S(1)}, bf16[512,1024]{1,0:T(8,128)(2,1)}, u32[]{:S(2)}) copy-start(bf16[512,1024]{1,0:T(8,128)(2,1)} %param.21) | copy-start | bytes 3145732
  451.4 61.8 %copy-start.25 = (f32[512]{0:T(512)S(1)}, f32[512]{0:T(512)}, u32[]{:S(2)}) copy-start(f32[512]{0:T(512)} %copy-done.24) | copy-start | bytes 6148
  451.4 61.8 %copy-start.27 = (f32[512]{0:T(512)S(1)}, f32[512]{0:T(512)}, u32[]{:S(2)}) copy-start(f32[512]{0:T(512)} %copy-done.26) | copy-start | bytes 6148
  518.2 282.6 %all-reduce.7.cloned.1.call-start = ((), (), s32[]{:S(2)}) async-start(), calls=%async_computation.7 | async-start | bytes 8388608 | tf_op jit(solution)/shard_map/psum | solution.py:150
  520.9 165.9 %copy-start.29 = (bf16[8,128]{1,0:T(8,128)(2,1)S(1)}, bf16[8,128]{1,0:T(8,128)(2,1)}, u32[]{:S(2)}) copy-start(bf16[8,128]{1,0:T(8,128)(2,1)} %param.15) | copy-start | bytes 6148
  523.5 166.4 %copy-start.11 = (bf16[128,2048]{1,0:T(8,128)(2,1)S(1)}, bf16[128,2048]{1,0:T(8,128)(2,1)}, u32[]{:S(2)}) copy-start(bf16[128,2048]{1,0:T(8,128)(2,1)} %param.18) | copy-start | bytes 1572868
  688.6 117.7 %copy-start.20 = (f32[512,512]{1,0:T(8,128)S(1)}, f32[512,512]{1,0:T(8,128)}, u32[]{:S(2)}) copy-start(f32[512,512]{1,0:T(8,128)} %get-tuple-element.134) | copy-start | bytes 3145732
  800.8 6.6 copy-start.15
  (13 other events, 30.4 us)
Sparse Core Ops, SparseCore 0:
  160.2 33.1 all-gather.2
  194.9 21.2 all-gather.4
  225.4 31.8 reduce-scatter.4
  260.1 31.8 reduce-scatter.2
  518.4 166.9 all-reduce.4
  690.5 110.2 all-reduce.6
where the time goes:
time: 822 us; the launch traced here: 817 us
  waiting for transfers between devices  357 us (43%)
  local copies, waits for them, and re-layouts  143 us (17%)
  other arithmetic  141 us (17%)
  blocking collectives  94.2 us (11%)
  matrix products  55.4 us (7%)
  between operations  14.9 us (2%)
  starting transfers between devices  11.1 us (1%)
    psum x1, waiting for transfers between devices, shards(): lax.psum((up_share, upb_share, down_share), 'rows')  109 us
    scatter-add x1, other arithmetic, attend_back(): table_grad.at[index_part.reshape(-1)]  72.1 us
    psum x1, waiting for transfers between devices, shards(): lax.psum((query_share, keyval_share, output_share, modulation_share, jnp....  67.6 us
    psum x1, blocking collectives, shards(): lax.psum((up_share, upb_share, down_share), 'rows')  57 us
    ppermute x2, waiting for transfers between devices, shifted(): return lax.ppermute(x, axis, [(i, (i + by) % peers) for i in range(peers)])  56.3 us
    unnamed x81, local copies, waits for them, and re-layouts  55.4 us
    gather x1, local copies, waits for them, and re-layouts, attend(): kv_table[index_part]  42.8 us
    psum x1, blocking collectives, shards(): lax.psum((query_share, keyval_share, output_share, modulation_share, jnp....  37.2 us
  transfers between devices with their start and end apart: 10, of which 9 were waited for; matrix products, arithmetic and copies ran while one was open for 6% of the time, Pallas kernels for 0%

commit v1 on v0

v1 whole, which is shorter than its diff:
```python
import functools
import math
from types import SimpleNamespace

import jax
import jax.numpy as jnp
from jax import lax
from jax.experimental import pallas as pl
from jax.experimental.pallas import tpu as pltpu
from jax.sharding import PartitionSpec as P

HEADS = 4
EPSILON = 1e-05
MESH = pl.DeviceIdType.MESH
F32, BF = jnp.float32, jnp.bfloat16
PRECISE = lax.Precision.HIGHEST
NN = (((1,), (0,)), ((), ()))
NT = (((1,), (1,)), ((), ()))
TN = (((0,), (0,)), ((), ()))
MASKED = -1e30


def dot(a, b, dims=NN, precision=None):
    return lax.dot_general(a, b, dims, precision=precision, preferred_element_type=F32)


def mean(v):
    return jnp.mean(v, axis=-1, keepdims=True)


def layer_norm(values):
    centred = values - mean(values)
    inverse = lax.rsqrt(mean(centred * centred) + EPSILON)
    return centred * inverse, inverse


def norm_back(grad, normed, inverse):
    return inverse * (grad - mean(grad) - normed * mean(grad * normed))


def iota(shape, axis):
    return lax.broadcasted_iota(jnp.int32, shape, axis)


def loop(count, body):
    lax.fori_loop(0, count, lambda i, c: (body(i), c)[1], 0)


def remote(src, dst, sems, index, device):
    send, recv = sems
    return pltpu.make_async_remote_copy(
        src_ref=src,
        dst_ref=dst,
        send_sem=send.at[index],
        recv_sem=recv.at[index],
        device_id=device,
        device_id_type=MESH,
    )


class Sum:
    def __init__(self, out, dtype, bufs, sems, base, place, over_mlp):
        self.part, self.out, self.dtype, self.bufs = bufs.part, out, dtype, bufs
        self.sems, self.base, self.over_mlp = sems, base, over_mlp
        self.r, self.m, self.M, self.core, self.x, self.z, self.nz = place
        self.rows, cols = out.shape
        self.half = self.rows // 2
        self.piece = self.half // self.nz
        self.width = cols // 2
        self.mine = pl.ds(pl.multiple_of(self.core * self.width, self.width), self.width)
        self.other = pl.ds(pl.multiple_of((1 - self.core) * self.width, self.width), self.width)
        self.sent = []

    def row(self, z, x, core):
        return z * 4 + x * 2 + core

    def copy(self, src, dst, slot, row, m):
        c = remote(src, dst, self.sems, self.base + slot, (row, m))
        c.start()
        if slot > 0:
            self.sent.append(c)
        return c

    def cut(self, start, size):
        return pl.ds(pl.multiple_of(start, size), size)

    def core_send(self):
        b = self.bufs
        self.c_core = self.copy(b.cs, b.cr, 0, self.row(self.z, self.x, 1 - self.core), self.m)

    def x_send(self):
        b = self.bufs
        self.c_core.wait()
        rows = self.cut((1 - self.x) * self.half, self.half)
        stage = b.cs.at[0 : self.half]
        stage[...] = (self.part[rows, :] + b.cr[rows, :].astype(F32)).astype(self.dtype)
        self.c_x = self.copy(stage, b.xr, 1, self.row(self.z, 1 - self.x, self.core), self.m)

    def z_send(self):
        b = self.bufs
        self.c_x.wait_recv()
        rows = self.cut(self.x * self.half, self.half)
        value = self.part[rows, :] + b.cr[rows, :].astype(F32) + b.xr[...].astype(F32)
        self.part[rows, :] = value
        stage = b.cs.at[self.half :]
        stage[...] = value.astype(self.dtype)
        self.c_z = []
        for t in range(1, self.nz):
            to = lax.rem(self.z + t, self.nz)
            self.c_z.append(
                self.copy(
                    b.cs.at[self.cut(self.half + to * self.piece, self.piece)],
                    b.zr.at[t - 1],
                    1 + t,
                    self.row(to, self.x, self.core),
                    self.m,
                )
            )

    def z_sum(self):
        b = self.bufs
        value = self.part[self.cut(self.x * self.half + self.z * self.piece, self.piece), :]
        for t in range(1, self.nz):
            self.c_z[t - 1].wait_recv()
            value = value + b.zr[t - 1].astype(F32)
        return value

    def m_send(self):
        b = self.bufs
        b.mr[self.m] = self.z_sum().astype(self.dtype)
        self.c_m = []
        for t in range(1, self.M):
            self.c_m.append(
                self.copy(
                    b.mr.at[self.m],
                    b.mr.at[self.m],
                    self.nz + t,
                    self.r,
                    lax.rem(self.m + t, self.M),
                )
            )

    def z_gather(self):
        b = self.bufs
        if self.over_mlp:
            for c in self.c_m:
                c.wait_recv()
            value = b.mr[0].astype(F32)
            for t in range(1, self.M):
                value = value + b.mr[t].astype(F32)
        else:
            value = self.z_sum()
        here = (self.cut(self.x * self.half + self.z * self.piece, self.piece), self.mine)
        self.out[here[0], here[1]] = value.astype(self.dtype)
        block = self.out.at[here[0], here[1]]
        first = self.nz + self.M
        self.c_gz = []
        for t in range(1, self.nz):
            to = lax.rem(self.z + t, self.nz)
            self.c_gz.append(
                self.copy(block, block, first + t - 1, self.row(to, self.x, self.core), self.m)
            )

    def x_gather(self):
        for c in self.c_gz:
            c.wait_recv()
        block = self.out.at[self.cut(self.x * self.half, self.half), self.mine]
        slot = 2 * self.nz + self.M - 1
        self.c_gx = self.copy(block, block, slot, self.row(self.z, 1 - self.x, self.core), self.m)

    def core_gather(self):
        self.c_gx.wait_recv()
        block = self.out.at[:, self.mine]
        slot = 2 * self.nz + self.M
        self.c_gc = self.copy(block, block, slot, self.row(self.z, self.x, 1 - self.core), self.m)

    def finish(self):
        self.c_gc.wait_recv()
        for c in self.sent:
            c.wait_send()

    @staticmethod
    def slots(nz, m):
        return 2 * nz + m + 1


SUMS = ("up", "down", "out", "query", "keyval", "tail")
BUFFERS = ("part", "cs", "cr", "xr", "zr", "mr")


def kernel(static, names, *refs):
    ref = SimpleNamespace(**dict(zip(names, refs)))
    R, M, rows, D, F, S, near = static
    nz = R // 4
    G = rows // S
    W = 3 * G
    head = D // HEADS
    factor = 1.0 / math.sqrt(head)
    r, y = lax.axis_index("rows"), lax.axis_index("mlp")
    core, xi, z = lax.rem(r, 2), lax.rem(r // 2, 2), r // 4
    me = r * M + y
    devices = R * M
    pairs = M == 2
    up_row, down_row = lax.rem(r + 1, R), lax.rem(r + R - 1, R)
    after, before = lax.rem(me + 1, devices), lax.rem(me + devices - 1, devices)

    local = []
    lsem = ref.lsem
    for i, (src, dst) in enumerate(
        (
            (ref.x, ref.xb.at[1]),
            (ref.wq, ref.wqkv.at[:, 0:D]),
            (ref.wkv, ref.wqkv.at[:, D : 3 * D]),
            (ref.cot, ref.cotn),
            (ref.wo, ref.wob),
            (ref.wup, ref.wupb),
            (ref.wdn, ref.wdnb),
        )
    ):
        c = pltpu.make_async_copy(src, dst, lsem.at[i])
        c.start()
        local.append(c)

    barrier = pltpu.get_barrier_semaphore()
    others = [(r, lax.rem(y + t, M)) for t in range(1, M)]
    others.append((z * 4 + xi * 2 + 1 - core, y))
    others.append((z * 4 + (1 - xi) * 2 + core, y))
    for t in range(1, nz):
        others.append((lax.rem(z + t, nz) * 4 + xi * 2 + core, y))
    if pairs:
        others += [(up_row, y), (down_row, y)]
    else:
        others += [(after // M, lax.rem(after, M)), (before // M, lax.rem(before, M))]
    for device in others:
        pl.semaphore_signal(barrier, inc=1, device_id=device, device_id_type=MESH)
    pl.semaphore_wait(barrier, len(others))

    def halo(source, at, sems):
        def first(k):
            if pairs:
                return [remote(source(k), at(2 * y, k), sems, (0, k), (r, 1 - y))]
            return [
                remote(source(k), at(0, k), sems, (0, k), (after // M, lax.rem(after, M))),
                remote(source(k), at(2, k), sems, (1, k), (before // M, lax.rem(before, M))),
            ]

        def second(k):
            if pairs:
                to = jnp.where(y == 0, up_row, down_row)
                return remote(at(2 * (1 - y), k), at(2 * y, k), sems, (1, k), (to, y))
            return first(k)[1]

        def send(k):
            for c in first(k):
                c.start()

        def pass_on(k):
            first(k)[0].wait_recv()
            if pairs:
                second(k).start()

        def arrive(k):
            second(k).wait_recv()

        def drain(k):
            first(k)[0].wait_send()
            second(k).wait_send()

        return send, pass_on, arrive, drain

    near_slot = 2 * (1 - y) if pairs else 0
    far_slot = 2 * y if pairs else 2
    xb = ref.xb
    quarter = rows // 4

    def part(k, n=quarter):
        return pl.ds(pl.multiple_of(k * n, n), n)

    x_send, x_pass, x_arrive, x_drain = halo(
        lambda k: ref.x.at[part(k)], lambda slot, k: xb.at[slot, part(k)], ref.xsem
    )
    loop(4, x_send)

    def build(k):
        at = part(k)
        a, b = iota((quarter, rows), 0) + k * quarter, iota((quarter, rows), 1)
        ref.pm[at, :] = jnp.where(b == lax.rem(a, G) * S + a // G, 1.0, 0.0).astype(BF)
        ref.pt[at, :] = jnp.where(a == lax.rem(b, G) * S + b // G, 1.0, 0.0).astype(BF)

    loop(4, build)
    pm, pt = ref.pm, ref.pt

    nodes = devices * G
    place = ref.nbr[...] // S - me * G + G
    place = jnp.where(place < 0, place + nodes, place)
    place = jnp.where(place >= nodes, place - nodes, place)
    place = place.astype(F32).astype(BF)
    lws = ref.lws
    lws[rows : rows + G, :] = jnp.zeros((G, near), F32)
    lws[0:rows, :] = dot(pm[...], place)
    lwt = ref.lwt
    eye = jnp.where(iota((near, near), 0) == iota((near, near), 1), 1.0, 0.0).astype(BF)

    def turn(s):
        block = lws[pl.ds(pl.multiple_of(s * G, G), 2 * G), :].astype(BF)
        lwt[1, s] = dot(eye, block, NT).astype(BF)

    loop(S, turn)
    l_send, l_pass, l_arrive, l_drain = halo(
        lambda k: lwt.at[1], lambda slot, k: lwt.at[slot], ref.lwsem
    )
    l_send(0)

    modulation = dot(ref.nc[...], ref.adaw[...]) + ref.adab[...].astype(F32)
    ref.mod[...] = modulation
    mods = ref.mods
    for s in range(S):
        mods[s : s + 1, :] = ref.mod[pl.ds(ref.sid[s], 1), :]

    n1n, n1s, qkv = ref.n1n, ref.n1s, ref.qkv
    wqkv = ref.wqkv

    def norm_block(slot, k):
        at = part(k)
        normed, _ = layer_norm(xb[slot, at, :].astype(F32))
        scaled = normed.reshape(quarter // S, S, D) * (1.0 + mods[:, 0:D])[None]
        scaled = scaled + mods[:, D : 2 * D][None]
        n1n[at, :] = scaled.reshape(quarter, D).astype(BF)

    def project(slot, k):
        ordered = dot(pm[part(k), :], n1n[...]).astype(BF)
        wide = dot(ordered, wqkv[...]).astype(BF)
        two = quarter // G
        qkv[pl.ds(two * k, two), pl.ds(pl.multiple_of(slot * G, G), G), :] = wide.reshape(
            two, G, 3 * D
        )
        return ordered

    local[0].wait()
    loop(4, lambda k: norm_block(1, k))
    local[1].wait()
    local[2].wait()

    def own_project(k):
        n1s[part(k), :] = project(1, k)

    loop(4, own_project)
    local[3].wait()
    xs, cotb = ref.xs, ref.cotb

    def order(k):
        xs[part(k), :] = dot(pm[part(k), :], xb[1]).astype(BF)
        cotb[y, part(k), :] = dot(pm[part(k), :], ref.cotn[...]).astype(BF)

    loop(4, order)

    cnt, cntt = ref.cnt, ref.cntt

    def count(s):
        block = lws[pl.ds(pl.multiple_of(s * G, G), G), :].astype(jnp.int32)
        lane = iota((G, W), 1)
        total = jnp.zeros((G, W), F32)
        for j in range(near):
            total = total + jnp.where(block[:, j : j + 1] == lane, 1.0, 0.0)
        cnt[s] = total

    loop(S, count)

    def near_norm(k):
        x_pass(k)
        norm_block(near_slot, k)

    loop(4, near_norm)
    l_pass(0)

    half = rows // 2

    def mlp_copies(buf, sems, k, n):
        block = buf.at[y, part(k, n)]
        return [
            remote(block, block, sems, (t - 1, k), (r, lax.rem(y + t, M))) for t in range(1, M)
        ]

    def start_all(copies):
        for c in copies:
            c.start()

    loop(2, lambda k: start_all(mlp_copies(cotb, ref.cotsem, k, half)))
    loop(4, lambda k: project(near_slot, k))

    def far_norm(k):
        x_arrive(k)
        norm_block(far_slot, k)

    loop(4, far_norm)
    l_arrive(0)
    loop(4, lambda k: project(far_slot, k))

    mixs, mixx, prob, lsec = ref.mixs, ref.mixx, ref.prob, ref.lsec
    ntb, mid = ref.ntb, ref.mid
    local[4].wait()
    wo = ref.wob

    def attend(k):
        def sample(s2):
            s = 2 * k + s2
            at = pl.ds(pl.multiple_of(s * G, G), G)
            times = cnt[s]
            lane = iota((G, 128), 1)
            logs = jnp.zeros((G, 128), F32)
            for h in range(HEADS):
                lo, hi = h * head, (h + 1) * head
                scores = dot(qkv[s, G : 2 * G, lo:hi], qkv[s, :, D + lo : D + hi], NT) * factor
                scores = jnp.where(times > 0.0, scores, MASKED)
                top = jnp.max(scores, axis=-1, keepdims=True)
                power = jnp.exp(scores - top)
                total = jnp.sum(power * times, axis=-1, keepdims=True)
                probs = power * (1.0 / total)
                prob[s * HEADS + h] = probs
                weight = (times * probs.astype(BF).astype(F32)).astype(BF)
                rest = (times * probs - weight.astype(F32)).astype(BF)
                values = qkv[s, :, 2 * D + lo : 2 * D + hi]
                mixed = dot(weight, values)
                mixs[at, lo:hi] = mixed.astype(BF)
                mixx[at, lo:hi] = mixed + dot(rest, values)
                logs = jnp.where(lane == h, top + jnp.log(total), logs)
            lsec[at, :] = logs

        loop(2, sample)
        middle = xs[part(k), :].astype(F32) + dot(mixs[part(k), :], wo[...])
        mid[part(k), :] = middle
        normed, _ = layer_norm(middle)
        for s2 in range(2):
            at = pl.ds(pl.multiple_of(k * quarter + s2 * G, G), G)
            scale = mods[pl.ds(2 * k + s2, 1), 2 * D : 3 * D]
            shift = mods[pl.ds(2 * k + s2, 1), 3 * D : 4 * D]
            ntb[y, at, :] = (normed[s2 * G : (s2 + 1) * G] * (1.0 + scale) + shift).astype(BF)
        start_all(mlp_copies(ntb, ref.ntsem, k, quarter))

    loop(4, attend)

    local[5].wait()
    local[6].wait()
    wup, wdn, actb, ghb = ref.wupb, ref.wdnb, ref.actb, ref.ghb
    bupg, g2s, g2r, g2o = ref.bupg, ref.g2s, ref.g2r, ref.g2o
    brr = ref.brr
    bupg[...] = jnp.zeros_like(bupg)
    tile = 256

    def back_copy(src, dst, sems, j, c):
        owner = lax.rem(y + 2 * M - 1 - j, M)
        return remote(src.at[j, part(c, half)], dst.at[j, part(c, half)], sems, (j, c), (r, owner))

    def feed(i):
        j, c = i // 2, lax.rem(i, 2)
        slot = lax.rem(y + 2 * M - 1 - j, M)
        away = j < M - 1

        @pl.when(away)
        def _():
            for q in range(2):
                k = 2 * c + q
                block = ntb.at[slot, part(k)]
                remote(block, block, ref.ntsem, (j, k), (r, y)).wait_recv()
            block = cotb.at[slot, part(c, half)]
            remote(block, block, ref.cotsem, (j, c), (r, y)).wait_recv()

        at = part(c, half)
        flat = pl.ds(pl.multiple_of(slot * rows + c * half, half), half)

        def column(f):
            cols = part(f, tile)
            hidden = dot(ntb[slot, at, :], wup[:, cols]) + ref.bup[:, cols].astype(F32)
            gate = jax.nn.sigmoid(hidden)
            actb[flat, cols] = (hidden * gate).astype(BF)
            grad = dot(cotb[slot, at, :], wdn[cols, :], NT)
            grad = (grad * gate * (1.0 + hidden * (1.0 - gate))).astype(BF)
            ghb[flat, cols] = grad
            bupg[:, cols] += jnp.sum(grad.astype(F32), axis=0, keepdims=True)

        loop(F // tile, column)
        for q in range(D // tile):
            lo, hi = q * tile, (q + 1) * tile
            two = dot(ghb[flat, :], wup[lo:hi, :], NT)

            @pl.when(away)
            def _():
                jj = jnp.minimum(j, M - 2)
                g2s[jj, at, lo:hi] = two.astype(BF)

            @pl.when(jnp.logical_not(away))
            def _():
                g2o[at, lo:hi] = two

        @pl.when(away)
        def _():
            back_copy(g2s, g2r, ref.g2sem, j, c).start()

    loop(2 * M, feed)

    place_of = (r, y, M, core, xi, z, nz)
    count_of = Sum.slots(nz, M)
    sums = SimpleNamespace()
    targets = (ref.o_up, ref.o_dn, ref.o_out, ref.o_q, ref.o_kv, ref.tailo)
    for i, (name, out, bufs) in enumerate(zip(SUMS, targets, ref.sums)):
        bufs = SimpleNamespace(**dict(zip(BUFFERS, bufs)))
        dtype = F32 if out is ref.tailo else BF
        total = Sum(out, dtype, bufs, ref.sumsem, i * count_of, place_of, i > 1)
        setattr(sums, name, total)

    def weight_grad(total, left, right):
        rows_of, width = total.rows, total.width
        step = min(tile, width)
        for out, start, kind in (
            (total.bufs.cs, (1 - core) * width, BF),
            (total.part, core * width, F32),
        ):

            def tile_row(a):
                lhs = left(a)

                def column(f):
                    at = pl.ds(pl.multiple_of(start + f * step, step), step)
                    out[part(a, tile), part(f, step)] = dot(lhs, right(at), TN).astype(kind)

                loop(width // step, column)

            loop(rows_of // tile, tile_row)
            if kind == BF:
                total.core_send()

    weight_grad(
        sums.up,
        lambda a: ntb[:, :, part(a, tile)].reshape(M * rows, tile),
        lambda at: ghb[:, at],
    )
    weight_grad(
        sums.down,
        lambda a: actb[:, part(a, tile)],
        lambda at: cotb[:, :, at].reshape(M * rows, at.size),
    )

    gmid, gmw, stw, gatt, gmod = ref.gmid, ref.gmw, ref.stw, ref.cotn, ref.gmod
    pick_log = jnp.where(
        (iota((8, 128), 0) == iota((8, 128), 1)) & (iota((8, 128), 0) < HEADS), 1.0, 0.0
    )
    pick_head = jnp.where(iota((8, D), 0) == iota((8, D), 1) // head + HEADS, 1.0, 0.0)
    m_send, m_pass, m_arrive, m_drain = halo(
        lambda k: gmw.at[pl.ds(2 * k, 2), pl.ds(G, G)],
        lambda slot, k: gmw.at[pl.ds(2 * k, 2), pl.ds(pl.multiple_of(slot * G, G), G)],
        ref.gmsem,
    )
    s_send, s_pass, s_arrive, s_drain = halo(
        lambda k: stw.at[1, pl.ds(2 * k, 2)],
        lambda slot, k: stw.at[slot, pl.ds(2 * k, 2)],
        ref.stsem,
    )

    def middle_back(k):
        @pl.when(lax.rem(k, 2) == 0)
        def _():
            for j in range(M - 1):
                back_copy(g2s, g2r, ref.g2sem, j, k // 2).wait_recv()

        at = part(k)
        grad = g2o[at, :]
        for j in range(M - 1):
            grad = grad + g2r[j, at, :].astype(F32)
        normed, inverse = layer_norm(mid[at, :])
        weighted = []
        for s2 in range(2):
            s = 2 * k + s2
            lo, hi = s2 * G, (s2 + 1) * G
            scale = mods[pl.ds(s, 1), 2 * D : 3 * D]
            weighted.append(grad[lo:hi] * (1.0 + scale))
            gmod[pl.ds(s, 1), 2 * D : 3 * D] = jnp.sum(
                grad[lo:hi] * normed[lo:hi], axis=0, keepdims=True
            )
            gmod[pl.ds(s, 1), 3 * D : 4 * D] = jnp.sum(grad[lo:hi], axis=0, keepdims=True)
        weighted = jnp.concatenate(weighted, axis=0)
        middle = cotb[y, at, :].astype(F32) + norm_back(weighted, normed, inverse)
        gmid[at, :] = middle
        rounded = middle.astype(BF)
        gatt[at, :] = rounded
        mixture = dot(rounded, wo[...], NT).astype(BF)
        gmw[pl.ds(2 * k, 2), G : 2 * G, :] = mixture.reshape(2, G, D)
        product = mixture.astype(F32) * mixx[at, :]
        stats = dot(pick_log, lsec[at, :], NT, PRECISE) + dot(pick_head, product, NT, PRECISE)
        stw[1, 2 * k] = stats
        stw[1, 2 * k + 1] = pltpu.roll(stats, G, 1)
        m_send(k)
        s_send(k)

    loop(4, middle_back)
    sums.up.x_send()
    sums.down.x_send()

    def branch_copy(j, c):
        owner = lax.rem(y + 2 * M - 1 - j, M)
        at = part(c, half)
        return remote(ntb.at[owner, at], brr.at[j, at], ref.brsem, (j, c), (r, owner))

    def branch(i):
        j, c = i // 2, lax.rem(i, 2)
        slot = lax.rem(y + 2 * M - 1 - j, M)
        flat = pl.ds(pl.multiple_of(slot * rows + c * half, half), half)
        for q in range(D // tile):
            lo, hi = q * tile, (q + 1) * tile
            ntb[slot, part(c, half), lo:hi] = dot(actb[flat, :], wdn[:, lo:hi]).astype(BF)
        branch_copy(j, c).start()

    loop(2 * (M - 1), branch)

    weight_grad(sums.out, lambda a: mixs[:, part(a, tile)], lambda at: gatt[:, at])

    gqkv = ref.gqkv

    def query_back(s):
        at = pl.ds(pl.multiple_of(s * G, G), G)
        times = cnt[s]
        for h in range(HEADS):
            lo, hi = h * head, (h + 1) * head
            grad = gmw[s, G : 2 * G, lo:hi]
            delta = jnp.sum(grad.astype(F32) * mixx[at, lo:hi], axis=-1, keepdims=True)
            gprob = dot(grad, qkv[s, :, 2 * D + lo : 2 * D + hi], NT)
            gscore = (prob[s * HEADS + h] * (gprob - delta)).astype(BF).astype(F32)
            weight = (times * gscore).astype(BF)
            gqkv[at, lo:hi] = (dot(weight, qkv[s, :, D + lo : D + hi]) * factor).astype(BF)

    def query_pass(s):
        query_back(s)

        @pl.when(s >= 4)
        def _():
            m_pass(s - 4)
            s_pass(s - 4)

    loop(S, query_pass)

    weight_grad(sums.query, lambda a: n1s[:, part(a, tile)], lambda at: gqkv[:, at])
    sums.out.x_send()

    def count_back(s):
        shift = [2 * G, G, 0]
        block = jnp.concatenate(
            [lwt[b, s][:, 0:G].astype(F32) - float(shift[b]) for b in range(3)], axis=1
        ).astype(jnp.int32)
        key = iota((G, W), 0)
        total = jnp.zeros((G, W), F32)
        for j in range(near):
            total = total + jnp.where(block[j : j + 1, :] == key, 1.0, 0.0)
        cntt[s] = total

    loop(S, count_back)
    sums.up.z_send()
    sums.down.z_send()

    def key_back(s):
        @pl.when(lax.rem(s, 2) == 0)
        def _():
            m_arrive(s // 2)
            s_arrive(s // 2)

        at = pl.ds(pl.multiple_of(s * G, G), G)
        times = cntt[s]
        stats = jnp.concatenate([stw[b, s][:, 0:G] for b in range(3)], axis=1)
        for h in range(HEADS):
            lo, hi = h * head, (h + 1) * head
            queries = qkv[s, :, lo:hi]
            grads = gmw[s, :, lo:hi]
            scores = dot(qkv[s, G : 2 * G, D + lo : D + hi], queries, NT) * factor
            probs = jnp.exp(jnp.where(times > 0.0, scores - stats[h : h + 1], MASKED))
            gprob = dot(qkv[s, G : 2 * G, 2 * D + lo : 2 * D + hi], grads, NT)
            gscore = probs * (gprob - stats[HEADS + h : HEADS + h + 1])
            gscore = (times * gscore.astype(BF).astype(F32)).astype(BF)
            weight = (times * probs.astype(BF).astype(F32)).astype(BF)
            gqkv[at, D + lo : D + hi] = (dot(gscore, queries) * factor).astype(BF)
            gqkv[at, 2 * D + lo : 2 * D + hi] = dot(weight, grads).astype(BF)

    loop(S, key_back)

    keyval = gqkv.at[:, D : 3 * D]
    weight_grad(sums.keyval, lambda a: n1s[:, part(a, tile)], lambda at: keyval[:, at])
    sums.query.x_send()

    gdbs = ref.gdbs
    out_rows = ref.o_rows

    def first_back(s):
        at = pl.ds(pl.multiple_of(s * G, G), G)
        grad = dot(gqkv[at, :], wqkv[...], NT)
        normed, inverse = layer_norm(xs[at, :].astype(F32))
        gmod[pl.ds(s, 1), 0:D] = jnp.sum(grad * normed, axis=0, keepdims=True)
        gmod[pl.ds(s, 1), D : 2 * D] = jnp.sum(grad, axis=0, keepdims=True)
        gdbs[pl.ds(s, 1), :] = jnp.sum(cotb[y, at, :].astype(F32), axis=0, keepdims=True)
        weighted = grad * (1.0 + mods[pl.ds(s, 1), 0:D])
        g2o[at, :] = gmid[at, :] + norm_back(weighted, normed, inverse)

    loop(S, first_back)
    sums.keyval.x_send()

    tail, tailo = ref.tail, ref.tailo
    tail[...] = jnp.zeros_like(tail)
    for c in range(4 * D // tile):
        tail[c * S : (c + 1) * S, :] = gmod[:, c * tile : (c + 1) * tile]
    base = 4 * D // tile * S
    for c in range(D // tile):
        tail[base + c * S : base + (c + 1) * S, :] = gdbs[:, c * tile : (c + 1) * tile]
    base_up = base + D // tile * S
    for c in range(F // tile):
        tail[pl.ds(base_up + y * (F // tile) + c, 1), :] = bupg[:, c * tile : (c + 1) * tile]
    sums.tail.bufs.cs[...] = tail[:, sums.tail.other]
    sums.tail.part[...] = tail[:, sums.tail.mine]
    sums.tail.core_send()
    sums.out.z_send()
    sums.query.z_send()
    sums.tail.x_send()
    sums.up.z_gather()
    sums.down.z_gather()
    sums.keyval.z_send()
    sums.tail.z_send()
    sums.out.m_send()
    sums.query.m_send()

    for c in range(D // 128):
        lo, hi = c * 128, (c + 1) * 128
        for s in range(S):
            ref.turn[c, pl.ds(s, G, stride=S), :] = g2o[s * G : (s + 1) * G, lo:hi]
        out_rows[:, lo:hi] = ref.turn[c]

    sums.keyval.m_send()
    sums.tail.m_send()
    sums.up.x_gather()
    sums.down.x_gather()
    sums.out.z_gather()
    sums.query.z_gather()
    sums.keyval.z_gather()
    sums.tail.z_gather()

    def finish_out(k):
        @pl.when(lax.rem(k, 2) == 0)
        def _():
            for j in range(M - 1):
                branch_copy(j, k // 2).wait_recv()

        at = part(k)
        flat = pl.ds(pl.multiple_of(y * rows + k * quarter, quarter), quarter)
        value = mid[at, :] + dot(actb[flat, :], wdn[...]) + ref.bdn[...].astype(F32)
        for j in range(M - 1):
            value = value + brr[j, at, :].astype(F32)
        n1n[at, :] = value.astype(BF)

    loop(4, finish_out)

    def order_back(k):
        ref.o_layer[part(k), :] = dot(pt[part(k), :], n1n[...]).astype(BF)

    loop(4, order_back)

    sums.up.core_gather()
    sums.down.core_gather()
    late = (sums.out, sums.query, sums.keyval, sums.tail)
    for total in late:
        total.x_gather()
    for total in late:
        total.core_gather()
    sums.tail.finish()

    gms = ref.gms
    pick = jnp.zeros((S, S), F32)
    for s in range(S):
        hit = (iota((S, S), 1) == s) & (iota((S, S), 0) == ref.sid[s])
        pick = pick + jnp.where(hit, 1.0, 0.0)
    for c in range(4 * D // tile):
        gms[:, c * tile : (c + 1) * tile] = dot(
            pick, tailo[c * S : (c + 1) * S, :], NN, PRECISE
        )
    total = gms[...]
    ref.o_ada[...] = dot(ref.nc[...].astype(F32), total, TN, PRECISE)
    ref.o_adab[...] = jnp.sum(total, axis=0, keepdims=True)
    ref.o_cond[...] = dot(total, ref.adaw[...].astype(F32), NT, PRECISE)
    for c in range(D // tile):
        ref.o_downb[:, c * tile : (c + 1) * tile] = jnp.sum(
            tailo[base + c * S : base + (c + 1) * S, :], axis=0, keepdims=True
        )
    for c in range(F // tile):
        ref.o_upb[:, c * tile : (c + 1) * tile] = tailo[
            pl.ds(base_up + y * (F // tile) + c, 1), :
        ]

    for total in (sums.up, sums.down, sums.out, sums.query, sums.keyval):
        total.finish()

    loop(4, x_drain)
    l_drain(0)
    loop(4, m_drain)
    loop(4, s_drain)

    def drained(copies):
        for c in copies:
            c.wait_send()

    loop(2, lambda k: drained(mlp_copies(cotb, ref.cotsem, k, half)))
    loop(4, lambda k: drained(mlp_copies(ntb, ref.ntsem, k, quarter)))
    for j in range(M - 1):
        for c in range(2):
            back_copy(g2s, g2r, ref.g2sem, j, c).wait_send()
            branch_copy(j, c).wait_send()


def shards(
    node_rows,
    noise_cond,
    sample_id,
    neighbours,
    ada_weight,
    ada_bias,
    query_weight,
    keyval_weight,
    out_weight,
    up_weight,
    up_bias,
    down_weight,
    down_bias,
    cotangent,
):
    rows, D = node_rows.shape
    F = up_weight.shape[1]
    S, cond = noise_cond.shape
    near = neighbours.shape[1]
    R, M = lax.axis_size("rows"), lax.axis_size("mlp")
    nz = R // 4
    G = rows // S
    W = 3 * G
    small = 16 * nz if 16 * nz > 88 else 128
    V, H = pltpu.VMEM, pl.ANY
    shape = jax.ShapeDtypeStruct
    arguments = dict(
        x=(node_rows, H),
        nc=(noise_cond, V),
        sid=(sample_id, pltpu.SMEM),
        nbr=(neighbours, V),
        adaw=(ada_weight, V),
        adab=(ada_bias[None], V),
        wq=(query_weight, H),
        wkv=(keyval_weight, H),
        wo=(out_weight, H),
        wup=(up_weight, H),
        bup=(up_bias[None], V),
        wdn=(down_weight, H),
        bdn=(down_bias[None], V),
        cot=(cotangent, H),
    )
    outputs = dict(
        o_layer=shape((rows, D), BF),
        o_rows=shape((rows, D), F32),
        o_cond=shape((S, cond), F32),
        o_ada=shape((cond, 4 * D), F32),
        o_adab=shape((1, 4 * D), F32),
        o_q=shape((D, D), BF),
        o_kv=shape((D, 2 * D), BF),
        o_out=shape((D, D), BF),
        o_up=shape((D, F), BF),
        o_upb=shape((1, F), F32),
        o_dn=shape((F, D), BF),
        o_downb=shape((1, D), F32),
    )
    scratch = dict(
        xb=V((3, rows, D), BF),
        cotn=V((rows, D), BF),
        wqkv=V((D, 3 * D), BF),
        wob=V((D, D), BF),
        wupb=V((D, F), BF),
        wdnb=V((F, D), BF),
        pm=V((rows, rows), BF),
        pt=V((rows, rows), BF),
        lws=V((rows + G, near), F32),
        lwt=V((3, S, near, 2 * G), BF),
        mod=V((S, 4 * D), F32),
        mods=V((S, 4 * D), F32),
        n1n=V((rows, D), BF),
        n1s=V((rows, D), BF),
        xs=V((rows, D), BF),
        qkv=V((S, W, 3 * D), BF),
        cotb=V((M, rows, D), BF),
        cnt=V((S, G, W), F32),
        cntt=V((S, G, W), F32),
        mixs=V((rows, D), BF),
        mixx=V((rows, D), F32),
        prob=V((S * HEADS, G, W), F32),
        lsec=V((rows, 128), F32),
        ntb=V((M, rows, D), BF),
        mid=V((rows, D), F32),
        actb=V((M * rows, F), BF),
        ghb=V((M * rows, F), BF),
        bupg=V((1, F), F32),
        g2s=V((M - 1, rows, D), BF),
        g2r=V((M - 1, rows, D), BF),
        g2o=V((rows, D), F32),
        brr=V((M - 1, rows, D), BF),
        gmid=V((rows, D), F32),
        gmw=V((S, W, D), BF),
        stw=V((3, S, 8, 2 * G), F32),
        gmod=V((S, 4 * D), F32),
        gms=V((S, 4 * D), F32),
        gqkv=V((rows, 3 * D), BF),
        gdbs=V((S, D), F32),
        turn=V((D // 128, rows, 128), F32),
        tail=V((small, 256), F32),
        tailo=V((small, 256), F32),
    )
    sums = []
    for i, (n, c) in enumerate(((D, F), (F, D), (D, D), (D, D), (D, 2 * D), (small, 256))):
        dtype = F32 if i == 5 else BF
        bufs = [
            V((n, c // 2), F32),
            V((n, c // 2), dtype),
            V((n, c // 2), dtype),
            V((n // 2, c // 2), dtype),
            V((nz - 1, n // (2 * nz), c // 2), dtype),
        ]
        if i > 1:
            bufs.append(V((M, n // (2 * nz), c // 2), dtype))
        sums.append(tuple(bufs))
    scratch.update(sums=tuple(sums))
    sem = pltpu.SemaphoreType.DMA
    for name, dims in dict(
        xsem=(2, 4),
        lwsem=(2, 1),
        cotsem=(M - 1, 2),
        ntsem=(M - 1, 4),
        g2sem=(M - 1, 2),
        brsem=(M - 1, 2),
        gmsem=(2, 4),
        stsem=(2, 4),
        sumsem=(len(SUMS) * Sum.slots(nz, M),),
    ).items():
        scratch[name] = (sem(dims), sem(dims))
    scratch.update(lsem=sem((7,)))
    names = [*arguments, *outputs, *scratch]
    results = pl.pallas_call(
        functools.partial(kernel, (R, M, rows, D, F, S, near), names),
        out_shape=[*outputs.values()],
        in_specs=[pl.BlockSpec(memory_space=m) for _, m in arguments.values()],
        out_specs=[pl.BlockSpec(memory_space=V) for _ in outputs],
        scratch_shapes=[*scratch.values()],
        name="layer",
        compiler_params=pltpu.CompilerParams(
            collective_id=0, has_side_effects=True, vmem_limit_bytes=63 * 2**20
        ),
    )(*[a for a, _ in arguments.values()])
    got = SimpleNamespace(**dict(zip(outputs, results)))
    return (
        got.o_layer,
        got.o_rows,
        got.o_cond,
        got.o_ada,
        got.o_adab[0],
        got.o_q.astype(F32),
        got.o_kv.astype(F32),
        got.o_out.astype(F32),
        got.o_up.astype(F32),
        got.o_upb[0],
        got.o_dn.astype(F32),
        got.o_downb[0],
    )


def solution(mesh):
    both = P(("rows", "mlp"), None)
    placed = (
        both,
        P(),
        P(("rows", "mlp")),
        both,
        P(),
        P(),
        P(),
        P(),
        P(),
        P(None, "mlp"),
        P("mlp"),
        P("mlp", None),
        P(),
        both,
    )
    return jax.shard_map(
        shards,
        mesh=mesh,
        in_specs=placed,
        out_specs=(
            both,
            both,
            P(),
            P(),
            P(),
            P(),
            P(),
            P(),
            P(None, "mlp"),
            P("mlp"),
            P("mlp", None),
            P(),
        ),
        check_vma=False,
    )
```

time: 822 us -> 174 us (0.21)
  waiting for transfers between devices: 357 us -> 0 us
  Pallas kernels: 0 us -> 153 us
  local copies, waits for them, and re-layouts: 143 us -> 10.6 us
  other arithmetic: 141 us -> 9.21 us
  blocking collectives: 94.2 us -> 0 us
  matrix products: 55.4 us -> 0 us
  between operations: 14.9 us -> 0.68 us
  starting transfers between devices: 11.1 us -> 0 us
    psum x2 -> x0, waiting for transfers between devices: 176 us -> none  [the longest x1 109 us: shards(): lax.psum((up_share, upb_share, down_share), 'rows')]
    pallas_call x0 -> x1, Pallas kernels: none -> 153 us  [shards(): pl.pallas_call(functools.partial(kernel, (R, M, rows, D, F, S, near), nam...]
    psum x2 -> x0, blocking collectives: 94.2 us -> none  [the longest x1 57 us: shards(): lax.psum((up_share, upb_share, down_share), 'rows')]
    ppermute x4 -> x0, waiting for transfers between devices: 87.2 us -> none  [the longest x2 56.3 us: shifted(): return lax.ppermute(x, axis, [(i, (i + by) % peers) for i in range(peers)])]
    scatter-add x1 -> x0, other arithmetic: 72.1 us -> none  [attend_back(): table_grad.at[index_part.reshape(-1)]]
    dot_general x22 -> x0, matrix products: 55.4 us -> none  [the longest x16 35.4 us: bf_dot(): jnp.dot(left_operand, right_operand, preferred_element_type=jnp.float32)]
    all_gather x2 -> x0, waiting for transfers between devices: 49.7 us -> none  [the longest x1 32.3 us: shards(): gathered = lax.all_gather(normed_two, 'mlp', axis=0, tiled=True)]
    unnamed x81 -> x28, local copies, waits for them, and re-layouts: 55.4 us -> 6.73 us
  transfers between devices with their start and end apart: 10 -> 0, of which waited for: 9 -> 0; matrix products, arithmetic and copies ran while one was open for 6% -> 0% of each run, Pallas kernels for 0% -> 0%
where the time goes in v1:
time: 174 us
  Pallas kernels  153 us (88%)
  local copies, waits for them, and re-layouts  10.6 us (6%)
  other arithmetic  9.21 us (5%)
    pallas_call x1, Pallas kernels, shards(): pl.pallas_call(functools.partial(kernel, (R, M, rows, D, F, S, near), nam...  153 us
    unnamed x28, local copies, waits for them, and re-layouts  6.73 us

profile of v1, /device:TPU:0, one launch (start us, length us, event | category | flops | bytes accessed | tf_op | source)
XLA Modules:
  0.0 173.6 jit_solution(456643231045095281)
XLA Ops:
  0.6 1.3 broadcast_in_dim.11.refs_12_
  1.9 1.3 broadcast_in_dim.10.refs_10_
  3.2 1.3 broadcast_in_dim.9.refs_5_
  4.5 1.6 copy.26.refs_3_
  6.1 153.2 %layer.1 = (bf16[512,512]{1,0:T(8,128)(2,1)}, f32[512,512]{1,0:T(8,128)}, f32[8,128]{1,0:T(8,128)}, f32[128,2048]{1,0:T(8,128)}, f32[1,2048]{1,0:T(1,128)}, /*in...) custom-call(bf16[512,512]{1,0:T(8,128)(2,1)} %refs_0_.1, ...), custom_call_target="tpu_custom_call" | custom-call | tf_op jit(solution)/shard_map/layer/pallas_call | solution.py:941
  159.3 0.0 copy-start.2
  159.3 2.2 %convert_element_type.15 = f32[512,512]{1,0:T(8,128)} convert(bf16[512,512]{1,0:T(8,128)(2,1)} %get-tuple-element.29) | non-fusion elementwise | flops 262144 | bytes 1572864 | tf_op jit(solution)/shard_map/convert_element_type | solution.py:959
  161.5 0.0 copy-start.1
  161.5 2.2 %convert_element_type.17 = f32[512,512]{1,0:T(8,128)} convert(bf16[512,512]{1,0:T(8,128)(2,1)} %get-tuple-element.31) | non-fusion elementwise | flops 262144 | bytes 1572864 | tf_op jit(solution)/shard_map/convert_element_type | solution.py:961
  163.7 0.0 copy-done.2
  163.7 1.6 convert_element_type.16
  165.3 0.0 copy-done.1
  165.3 0.0 copy-start
  165.3 1.6 convert_element_type.18
  166.9 0.0 copy-done
  166.9 0.0 copy-start.5
  166.9 0.0 copy-start.4
  166.9 1.6 convert_element_type.19
  168.5 0.0 copy-done.5
  168.5 0.8 copy.34
  169.3 0.0 copy-done.4
  169.3 1.0 copy.35
  170.3 0.0 copy-done.8
  170.3 0.6 copy.36
  170.9 0.0 copy-done.3
  170.9 1.0 copy.37
  171.9 0.0 copy-done.6
  171.9 0.6 copy.38
  172.5 0.0 copy-done.7
  172.5 0.6 copy.39
  173.1 0.0 copy-done.9
  173.1 0.6 copy.40
  (5 shorter events, 0.0 us)
Async XLA Ops:
  159.3 4.5 %copy-start.2 = (bf16[512,1024]{1,0:T(8,128)(2,1)S(1)}, bf16[512,1024]{1,0:T(8,128)(2,1)}, u32[]{:S(2)}) copy-start(bf16[512,1024]{1,0:T(8,128)(2,1)} %get-tuple-element.30) | copy-start | bytes 3145732
  161.5 3.8 %copy-start.1 = (bf16[512,1024]{1,0:T(8,128)(2,1)S(1)}, bf16[512,1024]{1,0:T(8,128)(2,1)}, u32[]{:S(2)}) copy-start(bf16[512,1024]{1,0:T(8,128)(2,1)} %get-tuple-element.32) | copy-start | bytes 3145732
  165.3 1.6 copy-start
  166.9 1.6 copy-start.5
  166.9 2.4 %copy-start.4 = (f32[512,512]{1,0:T(8,128)S(1)}, f32[512,512]{1,0:T(8,128)}, u32[]{:S(2)}) copy-start(f32[512,512]{1,0:T(8,128)} %get-tuple-element.49) | copy-start | bytes 3145732
  168.5 1.8 %copy-start.8 = (f32[8,128]{1,0:T(8,128)S(1)}, f32[8,128]{1,0:T(8,128)}, u32[]{:S(2)}) copy-start(f32[8,128]{1,0:T(8,128)} %get-tuple-element.50) | copy-start | bytes 12292
  168.5 2.4 %copy-start.3 = (f32[128,2048]{1,0:T(8,128)S(1)}, f32[128,2048]{1,0:T(8,128)}, u32[]{:S(2)}) copy-start(f32[128,2048]{1,0:T(8,128)} %get-tuple-element.51) | copy-start | bytes 3145732
  169.3 2.6 %copy-start.6 = (f32[1,2048]{1,0:T(1,128)S(1)}, f32[1,2048]{1,0:T(1,128)}, u32[]{:S(2)}) copy-start(f32[1,2048]{1,0:T(1,128)} %get-tuple-element.28) | copy-start | bytes 24580
  169.3 3.2 %copy-start.7 = (f32[1,1024]{1,0:T(1,128)S(1)}, f32[1,1024]{1,0:T(1,128)}, u32[]{:S(2)}) copy-start(f32[1,1024]{1,0:T(1,128)} %get-tuple-element.33) | copy-start | bytes 12292
  169.3 3.7 %copy-start.9 = (f32[1,512]{1,0:T(1,128)S(1)}, f32[1,512]{1,0:T(1,128)}, u32[]{:S(2)}) copy-start(f32[1,512]{1,0:T(1,128)} %get-tuple-element.35) | copy-start | bytes 6148

commit v2 on v1

v2 whole, which is shorter than its diff:
```python
import functools
import math
from types import SimpleNamespace

import jax
import jax.numpy as jnp
from jax import lax
from jax.experimental import pallas as pl
from jax.experimental.pallas import tpu as pltpu
from jax.sharding import PartitionSpec as P

HEADS = 4
PAIRS = HEADS // 2
EPSILON = 1e-05
MESH = pl.DeviceIdType.MESH
F32, BF = jnp.float32, jnp.bfloat16
PRECISE = lax.Precision.HIGHEST
NN = (((1,), (0,)), ((), ()))
NT = (((1,), (1,)), ((), ()))
TN = (((0,), (0,)), ((), ()))
MASKED = -1e30


def dot(a, b, dims=NN, precision=None):
    return lax.dot_general(a, b, dims, precision=precision, preferred_element_type=F32)


def mean(v):
    return jnp.mean(v, axis=-1, keepdims=True)


def layer_norm(values):
    centred = values - mean(values)
    inverse = lax.rsqrt(mean(centred * centred) + EPSILON)
    return centred * inverse, inverse


def norm_back(grad, normed, inverse):
    return inverse * (grad - mean(grad) - normed * mean(grad * normed))


def iota(shape, axis):
    return lax.broadcasted_iota(jnp.int32, shape, axis)


def loop(count, body):
    lax.fori_loop(0, count, lambda i, c: (body(i), c)[1], 0)


def remote(src, dst, sems, index, device):
    send, recv = sems
    return pltpu.make_async_remote_copy(
        src_ref=src,
        dst_ref=dst,
        send_sem=send.at[index],
        recv_sem=recv.at[index],
        device_id=device,
        device_id_type=MESH,
    )


class Sum:
    def __init__(self, out, dtype, bufs, sems, base, place, order, role):
        self.out, self.dtype, self.sems, self.base = out, dtype, sems, base
        self.part, self.cs, self.cr, self.rr = bufs[:4]
        self.place = place
        self.order = order
        self.role = role
        self.all_sum = role == PLAIN and 0 not in order
        self.back = order if role != OTHERS else ()
        self.mr = bufs[4] if len(bufs) > 4 else None
        r, m, M, core, x, z, nz = place
        self.index = (m, x, z, x * nz + z)
        self.size = (M, 2, nz, 2 * nz)
        self.width = self.part.shape[1]
        self.mine = pl.ds(pl.multiple_of(core * self.width, self.width), self.width)
        self.other = pl.ds(pl.multiple_of((1 - core) * self.width, self.width), self.width)
        self.start, self.length, self.stage = [0], [self.part.shape[0]], [0]
        for axis in order:
            length = self.length[-1] // self.size[axis]
            self.start.append(self.start[-1] + self.index[axis] * length)
            self.stage.append(self.stage[-1] + self.length[-1] - length)
            self.length.append(length)
        if role != OTHERS:
            self.begin, self.extent = [0], [out.shape[0]]
            for axis in order:
                self.extent.append(self.extent[-1] // self.size[axis])
                self.begin.append(self.begin[-1] + self.index[axis] * self.extent[-1])
        self.todo = [functools.partial(self.share, i) for i in range(len(order))]
        if role == OTHERS:
            self.todo.append(self.send_over)
            return
        if self.all_sum:
            self.todo.append(self.send_mlp)
        self.todo.append(self.settle)
        self.todo += [functools.partial(self.gather, i) for i in reversed(range(len(self.back)))]
        self.todo.append(self.gather_core)

    def step(self, count=1):
        for _ in range(min(count, len(self.todo))):
            self.todo.pop(0)()

    def peer(self, axis, t):
        r, m, M, core, x, z, nz = self.place
        if axis == 0:
            return r, lax.rem(m + t, M)
        if axis == 1:
            return z * 4 + (1 - x) * 2 + core, m
        if axis == 2:
            return lax.rem(z + t, nz) * 4 + x * 2 + core, m
        to = lax.rem(x * nz + z + t, 2 * nz)
        return lax.rem(to, nz) * 4 + to // nz * 2 + core, m

    def slot(self, phase, axis, t):
        M, _, nz, _ = self.size
        return phase * (M + 3 * nz - 2) + (0, M - 1, M, M + nz - 1)[axis] + t - 1

    def copy(self, src, dst, slot, device):
        return remote(src, dst, self.sems, self.base + slot, device)

    def core_copy(self, phase):
        r, m, M, core, x, z, nz = self.place
        device = (z * 4 + x * 2 + 1 - core, m)
        slot = 2 * (M + 3 * nz - 2) + phase
        if phase == 0:
            return self.copy(self.cs, self.cr, slot, device)
        block = self.out.at[:, self.mine]
        return self.copy(block, block, slot, device)

    def share_copy(self, i, t):
        axis, length = self.order[i], self.length[i + 1]
        at = pl.ds(self.stage[i] + (t - 1) * length, length)
        return self.copy(
            self.cs.at[at], self.rr.at[at], self.slot(0, axis, t), self.peer(axis, t)
        )

    def gather_copy(self, i, t):
        axis = self.back[i]
        block = self.out.at[self.cut(self.begin[i + 1], self.extent[i + 1]), self.mine]
        return self.copy(block, block, self.slot(1, axis, t), self.peer(axis, t))

    def mlp_copy(self, t):
        r, m, M, core, x, z, nz = self.place
        block = self.mr.at[m]
        return self.copy(block, block, 2 * (M + 3 * nz - 2) + 1 + t, (r, lax.rem(m + t, M)))

    def cut(self, start, size):
        return pl.ds(pl.multiple_of(start, size), size)

    def core_send(self):
        self.core_copy(0).start()

    def take(self, i):
        if i == 0:
            self.core_copy(0).wait()
            return
        at = self.cut(self.start[i], self.length[i])
        value = self.part[at, :]
        for t in range(1, self.size[self.order[i - 1]]):
            self.share_copy(i - 1, t).wait_recv()
            here = pl.ds(self.stage[i - 1] + (t - 1) * self.length[i], self.length[i])
            value = value + self.rr[here, :].astype(F32)
        if i == 1:
            value = value + self.cr[at, :].astype(F32)
        self.part[at, :] = value

    def share(self, i):
        self.take(i)
        axis, length = self.order[i], self.length[i + 1]
        for t in range(1, self.size[axis]):
            block = lax.rem(self.index[axis] + t, self.size[axis])
            at = self.cut(self.start[i] + block * length, length)
            value = self.part[at, :]
            if i == 0:
                value = value + self.cr[at, :].astype(F32)
            self.cs[pl.ds(self.stage[i] + (t - 1) * length, length), :] = value.astype(self.dtype)
            self.share_copy(i, t).start()

    def send_mlp(self):
        n = len(self.order)
        self.take(n)
        r, m, M, core, x, z, nz = self.place
        self.mr[m] = self.part[self.cut(self.start[n], self.length[n]), :].astype(self.dtype)
        for t in range(1, M):
            self.mlp_copy(t).start()

    def over_copy(self, t):
        r, m, M, core, x, z, nz = self.place
        length = self.length[-1] // (M - 1)
        source = self.cs.at[pl.ds(self.stage[-1] + (t - 1) * length, length)]
        slot = 2 * (M + 3 * nz - 2) + 1 + t
        return self.copy(source, self.mate.mr.at[t - 1], slot, (r, lax.rem(m + t, M)))

    def send_over(self):
        n = len(self.order)
        self.take(n)
        value = self.part[self.cut(self.start[n], self.length[n]), :]
        self.cs[pl.ds(self.stage[n], self.length[n]), :] = value.astype(self.dtype)
        for t in range(1, self.size[0]):
            self.over_copy(t).start()

    def settle(self):
        n = len(self.order)
        at = self.cut(self.start[n], self.length[n])
        if self.all_sum:
            for t in range(1, self.size[0]):
                self.mlp_copy(t).wait_recv()
            value = self.mr[0].astype(F32)
            for t in range(1, self.size[0]):
                value = value + self.mr[t].astype(F32)
        else:
            self.take(n)
            value = self.part[at, :]
        if self.role == OWN:
            for t in range(1, self.size[0]):
                self.mate.over_copy(t).wait_recv()
                value = value + self.mr[t - 1].astype(F32)
        here = self.cut(self.begin[-1], self.extent[-1])
        self.out[here, self.mine] = value.astype(self.dtype)

    def gather(self, i):
        if i < len(self.back) - 1:
            for t in range(1, self.size[self.back[i + 1]]):
                self.gather_copy(i + 1, t).wait_recv()
        for t in range(1, self.size[self.back[i]]):
            self.gather_copy(i, t).start()

    def gather_core(self):
        for t in range(1, self.size[self.back[0]]):
            self.gather_copy(0, t).wait_recv()
        self.core_copy(1).start()

    def arrive(self):
        self.core_copy(1).wait_recv()

    def finish(self):
        assert not self.todo
        for i, axis in enumerate(self.order):
            for t in range(1, self.size[axis]):
                self.share_copy(i, t).wait_send()
        if self.role == OTHERS:
            for t in range(1, self.size[0]):
                self.over_copy(t).wait_send()
            return
        self.core_copy(1).wait_send()
        for i, axis in enumerate(self.back):
            for t in range(1, self.size[axis]):
                self.gather_copy(i, t).wait_send()
        if self.all_sum:
            for t in range(1, self.size[0]):
                self.mlp_copy(t).wait_send()

    @staticmethod
    def slots(nz, m):
        return 2 * (m + 3 * nz - 2) + 1 + m


class Spread:
    def __init__(self, source, parts, sems, base, place, z_first):
        self.source, self.parts, self.sems, self.base = source, parts, sems, base
        self.z_first = z_first
        self.place = place
        r, m, M, core, x, z, nz = place
        _, rows, cols = parts.shape
        self.rows, self.piece, width = rows, rows // (2 * nz), cols // 2
        self.mine = pl.ds(pl.multiple_of(core * width, width), width)
        self.here = self.cut((x * nz + z if z_first else z * 2 + x) * self.piece, self.piece)

    def cut(self, start, size):
        return pl.ds(pl.multiple_of(start, size), size)

    def copies(self, stage, t):
        r, m, M, core, x, z, nz = self.place
        base = self.base + (t - 1) * (nz + 2)
        if stage == 0:
            source = self.source.at[self.here, self.mine]
            target = self.parts.at[m, self.here, self.mine]
            return [remote(source, target, self.sems, base, (r, lax.rem(m + t, M)))]
        part = self.parts.at[lax.rem(m + M - t, M)]
        over_z = [lax.rem(z + u, nz) * 4 + x * 2 + core for u in range(1, nz)]
        over_x = [z * 4 + (1 - x) * 2 + core]
        if stage == 1:
            block = part.at[self.here, self.mine]
            rows = over_z if self.z_first else over_x
        elif stage == 2:
            many = (nz if self.z_first else 2) * self.piece
            block = part.at[self.cut((x if self.z_first else z) * many, many), self.mine]
            rows = over_x if self.z_first else over_z
        else:
            block = part.at[:, self.mine]
            rows = [z * 4 + x * 2 + 1 - core]
        first = base + (0, 1, nz if self.z_first else 2, nz + 1)[stage]
        return [
            remote(block, block, self.sems, first + i, (row, m)) for i, row in enumerate(rows)
        ]

    def each(self, stage):
        return [c for t in range(1, self.place[2]) for c in self.copies(stage, t)]

    def send(self, stage):
        if stage > 0:
            self.arrive(stage - 1)
        for c in self.each(stage):
            c.start()

    def arrive(self, stage):
        for c in self.each(stage):
            c.wait_recv()

    def drain(self):
        for stage in range(4):
            for c in self.each(stage):
                c.wait_send()


PLAIN, OWN, OTHERS = 0, 1, 2
SUMS = ("up", "down", "up2", "down2", "out", "query", "key", "value", "tail")
ROLES = (OWN, OWN, OTHERS, OTHERS, PLAIN, PLAIN, PLAIN, PLAIN, PLAIN)
FLAT, ALL = (1, 2), (0, 1, 2)
ORDERS = (FLAT, FLAT, FLAT, FLAT, ALL, ALL, ALL, (1, 2, 0), (0, 3))


def sharing(i, rows, M, nz):
    if rows % (16 * 2 * nz * M) == 0 or (i == len(SUMS) - 1 and rows % (8 * 2 * nz * M) == 0):
        return ORDERS[i]
    return tuple(axis for axis in ORDERS[i] if axis != 0)


def kernel(static, names, *refs):
    ref = SimpleNamespace(**dict(zip(names, refs)))
    R, M, rows, D, F, S, near = static
    nz = R // 4
    G = rows // S
    W = 3 * G
    head = D // HEADS
    factor = 1.0 / math.sqrt(head)
    r, y = lax.axis_index("rows"), lax.axis_index("mlp")
    core, xi, z = lax.rem(r, 2), lax.rem(r // 2, 2), r // 4
    me = r * M + y
    devices = R * M
    pairs = M == 2
    up_row, down_row = lax.rem(r + 1, R), lax.rem(r + R - 1, R)
    after, before = lax.rem(me + 1, devices), lax.rem(me + devices - 1, devices)

    local = []
    lsem = ref.lsem
    for i, (src, dst) in enumerate(
        (
            (ref.x, ref.xb.at[1]),
            (ref.wq, ref.wqkv.at[:, 0:D]),
            (ref.wkv, ref.wqkv.at[:, D : 3 * D]),
            (ref.cot, ref.cotn),
            (ref.wo, ref.wob),
            (ref.wup, ref.wupb.at[y]),
            (ref.wdn, ref.wdnb.at[y]),
        )
    ):
        c = pltpu.make_async_copy(src, dst, lsem.at[i])
        c.start()
        local.append(c)

    barrier = pltpu.get_barrier_semaphore()
    others = [(r, lax.rem(y + t, M)) for t in range(1, M)]
    others.append((z * 4 + xi * 2 + 1 - core, y))
    for t in range(1, 2 * nz):
        to = lax.rem(xi * nz + z + t, 2 * nz)
        others.append((lax.rem(to, nz) * 4 + to // nz * 2 + core, y))
    if pairs:
        others += [(up_row, y), (down_row, y)]
    else:
        others += [(after // M, lax.rem(after, M)), (before // M, lax.rem(before, M))]
    for device in others:
        pl.semaphore_signal(barrier, inc=1, device_id=device, device_id_type=MESH)
    pl.semaphore_wait(barrier, len(others))

    def halo(source, at, sems):
        def first(k):
            if pairs:
                return [remote(source(k), at(2 * y, k), sems, (0, k), (r, 1 - y))]
            return [
                remote(source(k), at(0, k), sems, (0, k), (after // M, lax.rem(after, M))),
                remote(source(k), at(2, k), sems, (1, k), (before // M, lax.rem(before, M))),
            ]

        def second(k):
            if pairs:
                to = jnp.where(y == 0, up_row, down_row)
                return remote(at(2 * (1 - y), k), at(2 * y, k), sems, (1, k), (to, y))
            return first(k)[1]

        def send(k):
            for c in first(k):
                c.start()

        def pass_on(k):
            first(k)[0].wait_recv()
            if pairs:
                second(k).start()

        def arrive(k):
            second(k).wait_recv()

        def drain(k):
            first(k)[0].wait_send()
            second(k).wait_send()

        return send, pass_on, arrive, drain

    near_slot = 2 * (1 - y) if pairs else 0
    far_slot = 2 * y if pairs else 2
    xb = ref.xb
    quarter = rows // 4

    def part(k, n=quarter):
        return pl.ds(pl.multiple_of(k * n, n), n)

    x_send, x_pass, x_arrive, x_drain = halo(
        lambda k: ref.x.at[part(k)], lambda slot, k: xb.at[slot, part(k)], ref.xsem
    )
    loop(4, x_send)
    place_of = (r, y, M, core, xi, z, nz)
    spread = [
        Spread(source, parts, ref.spsem, i * (M - 1) * (nz + 2), place_of, i == 0)
        for i, (source, parts) in enumerate(((ref.wup, ref.wupb), (ref.wdn, ref.wdnb)))
    ]
    for part_of in spread:
        part_of.send(0)
    upb = ref.upb
    upb[y] = jnp.broadcast_to(ref.bup[...].astype(F32).reshape(1, F), (8, F))

    def bias_copy(t):
        return remote(upb.at[y], upb.at[y], ref.ubsem, t - 1, (r, lax.rem(y + t, M)))

    for t in range(1, M):
        bias_copy(t).start()

    def build(k):
        at = part(k)
        a, b = iota((quarter, rows), 0) + k * quarter, iota((quarter, rows), 1)
        ref.pm[at, :] = jnp.where(b == lax.rem(a, G) * S + a // G, 1.0, 0.0).astype(BF)
        ref.pt[at, :] = jnp.where(a == lax.rem(b, G) * S + b // G, 1.0, 0.0).astype(BF)

    loop(4, build)
    a, b = iota((quarter, quarter), 0), iota((quarter, quarter), 1)
    few = quarter // S
    ref.pq[...] = jnp.where(b == lax.rem(a, few) * S + a // few, 1.0, 0.0).astype(BF)
    pm, pt = ref.pm, ref.pt

    nodes = devices * G
    place = ref.nbr[...] // S - me * G + G
    place = jnp.where(place < 0, place + nodes, place)
    place = jnp.where(place >= nodes, place - nodes, place)
    place = place.astype(F32).astype(BF)
    lws = ref.lws
    lws[rows : rows + G, :] = jnp.zeros((G, near), F32)
    lws[0:rows, :] = dot(pm[...], place, NT)
    lwt = ref.lwt
    eye = jnp.where(iota((near, near), 0) == iota((near, near), 1), 1.0, 0.0).astype(BF)

    def turn(s):
        block = lws[pl.ds(pl.multiple_of(s * G, G), 2 * G), :].astype(BF)
        lwt[1, s] = dot(eye, block, NT).astype(BF)

    loop(S, turn)
    l_send, l_pass, l_arrive, l_drain = halo(
        lambda k: lwt.at[1], lambda slot, k: lwt.at[slot], ref.lwsem
    )
    l_send(0)

    modulation = dot(ref.nc[...], ref.adaw[...]) + ref.adab[...].astype(F32).reshape(1, 4 * D)
    ref.mod[...] = modulation
    mods = ref.mods
    for s in range(S):
        mods[s : s + 1, :] = ref.mod[pl.ds(ref.sid[s], 1), :]

    n1s, qkv = ref.n1s, ref.qkv
    wqkv = ref.wqkv

    turn16 = quarter // S

    def norm_block(slot, k):
        at = part(k)
        normed, _ = layer_norm(xb[slot, at, :].astype(F32))
        scaled = normed.reshape(turn16, S, D) * (1.0 + mods[:, 0:D])[None]
        scaled = scaled + mods[:, D : 2 * D][None]
        ordered = dot(ref.pq[...], scaled.reshape(quarter, D).astype(BF)).astype(BF)
        wide = dot(ordered, wqkv[...]).astype(BF).reshape(S, turn16, 3 * D)
        here = pl.ds(pl.multiple_of(slot * G + k * turn16, turn16), turn16)
        qkv[:, here, :] = wide
        return ordered.reshape(S, turn16, D)

    local[0].wait()
    local[1].wait()
    local[2].wait()

    def own_norm(k):
        n1s[:, pl.ds(pl.multiple_of(k * turn16, turn16), turn16), :] = norm_block(1, k)

    loop(4, own_norm)
    local[3].wait()
    xs, cotb = ref.xs, ref.cotb

    def order(k):
        xs[part(k), :] = dot(pm[part(k), :], xb[1]).astype(BF)
        cotb[part(k), :] = dot(pm[part(k), :], ref.cotn[...]).astype(BF)

    loop(4, order)

    cnt, cntt = ref.cnt, ref.cntt

    def count(s):
        block = lwt[1, s].astype(F32)
        block = jnp.where(iota((near, 2 * G), 1) < G, block, pltpu.roll(block, G, 1))
        key = iota((W, 2 * G), 0).astype(F32)
        total = jnp.zeros((W, 2 * G), F32)
        for j in range(near):
            total = total + jnp.where(block[j : j + 1, :] == key, 1.0, 0.0)
        cnt[s] = total

    loop(S, count)

    def near_norm(k):
        x_pass(k)
        norm_block(near_slot, k)

    loop(4, near_norm)


    def far_norm(k):
        x_arrive(k)
        norm_block(far_slot, k)

        @pl.when(k == 2)
        def _():
            spread[0].send(1)
            spread[1].send(1)

    loop(4, far_norm)

    mixs, mixx, prob, stw = ref.mixs, ref.mixx, ref.prob, ref.stw
    ntb, mid = ref.ntb, ref.mid
    pair = 2 * head

    def apart(block):
        nothing = jnp.zeros((block.shape[0], head), block.dtype)
        left = jnp.concatenate([block[:, 0:head], nothing], axis=1)
        right = jnp.concatenate([nothing, block[:, head:pair]], axis=1)
        return jnp.concatenate([left, right], axis=0)

    def attend(k):
        for s2 in range(2):
            s = 2 * k + s2
            at = pl.ds(pl.multiple_of(s * G, G), G)
            times = cnt[s]
            logs = []
            for p in range(PAIRS):
                lo, hi = p * pair, (p + 1) * pair
                queries = apart(qkv[s, G : 2 * G, lo:hi])
                scores = dot(qkv[s, :, D + lo : D + hi], queries, NT) * factor
                scores = jnp.where(times > 0.0, scores, MASKED)
                top = jnp.max(scores, axis=0, keepdims=True)
                power = jnp.exp(scores - top)
                total = jnp.sum(power * times, axis=0, keepdims=True)
                probs = power * (1.0 / total)
                prob[s * PAIRS + p] = probs
                weight = (times * probs.astype(BF).astype(F32)).astype(BF)
                rest = (times * probs - weight.astype(F32)).astype(BF)
                both = jnp.concatenate([weight, rest], axis=1)
                mixed = dot(both, qkv[s, :, 2 * D + lo : 2 * D + hi], TN)
                one, two = mixed[0:G, 0:head], mixed[G : 2 * G, head:pair]
                mixs[at, lo : lo + head] = one.astype(BF)
                mixs[at, lo + head : hi] = two.astype(BF)
                mixx[at, lo : lo + head] = one + mixed[2 * G : 3 * G, 0:head]
                mixx[at, lo + head : hi] = two + mixed[3 * G : 4 * G, head:pair]
                logs.append(top + jnp.log(total))
            logs.append(jnp.zeros((8 - PAIRS, 2 * G), F32))
            stw[1, s] = jnp.concatenate(logs, axis=0)

    loop(4, attend)

    local[4].wait()
    wo = ref.wob
    half = rows // 2
    group = half // G

    def mix_out(c):
        at = part(c, half)
        middle = xs[at, :].astype(F32) + dot(mixs[at, :], wo[...])
        mid[at, :] = middle
        normed, _ = layer_norm(middle)
        for i in range(group):
            lo = i * G
            scale = mods[pl.ds(c * group + i, 1), 2 * D : 3 * D]
            shift = mods[pl.ds(c * group + i, 1), 3 * D : 4 * D]
            here = pl.ds(pl.multiple_of(c * half + lo, G), G)
            ntb[here, :] = (normed[lo : lo + G] * (1.0 + scale) + shift).astype(BF)

    loop(2, mix_out)

    local[5].wait()
    local[6].wait()
    l_pass(0)
    spread[0].send(2)
    spread[1].send(2)
    wup, wdn, actb, ghb = ref.wupb, ref.wdnb, ref.actb, ref.ghb
    bupg, g2o = ref.bupg, ref.g2o
    bupg[...] = jnp.zeros_like(bupg)
    g2o[...] = jnp.zeros_like(g2o)
    tile = 256

    def feed(p):
        def column(f):
            cols = part(f, tile)
            hidden = dot(ntb[...], wup[p, :, cols]) + upb[p, 0:1, cols]
            gate = jax.nn.sigmoid(hidden)
            active = hidden * gate
            actb[p, :, cols] = active.astype(BF)
            grad = dot(cotb[...], wdn[p, cols, :], NT)
            grad = (grad * (gate + active * (1.0 - gate))).astype(BF)
            ghb[p, :, cols] = grad
            bupg[p, 0:1, cols] += jnp.sum(grad.astype(F32), axis=0, keepdims=True)

        loop(F // tile, column)
        for q in range(D // tile):
            lo, hi = q * tile, (q + 1) * tile
            g2o[:, lo:hi] += dot(ghb[p], wup[p, lo:hi, :], NT)

    feed(y)

    count_of = Sum.slots(nz, M)
    sums = SimpleNamespace()
    written = []

    def write(source, result):
        c = pltpu.make_async_copy(source, result, ref.wsem.at[len(written)])
        c.start()
        written.append(c)

    for i, (name, bufs) in enumerate(zip(SUMS, ref.sums)):
        out, *bufs = bufs
        dtype = F32 if i == len(SUMS) - 1 else BF
        order = sharing(i, bufs[0].shape[0], M, nz)
        total = Sum(out, dtype, bufs, ref.sumsem, i * count_of, place_of, order, ROLES[i])
        setattr(sums, name, total)
    sums.up.mate, sums.down.mate, sums.up2.mate, sums.down2.mate = (
        sums.up2,
        sums.down2,
        sums.up,
        sums.down,
    )

    def weight_grad(total, left, right):
        width = total.width
        for out, start, kind in (
            (total.cs, (1 - core) * width, BF),
            (total.part, core * width, F32),
        ):
            at = pl.ds(pl.multiple_of(start, width), width)
            out[...] = dot(left, right(at), TN).astype(kind)
            if kind == BF:
                total.core_send()

    def ffn_grad(total, count, which, rows_of, left, right):
        width = total.width
        many, block = min(rows_of, 512), rows_of // (2 * nz)
        for out, start, kind in (
            (total.cs, (1 - core) * width, BF),
            (total.part, core * width, F32),
        ):
            at = pl.ds(pl.multiple_of(start, width), width)

            def tile_row(i):
                u, f = i // (rows_of // many), lax.rem(i, rows_of // many)
                p = which(u)
                value = dot(left(p, part(f, many)), right(p, at), TN).astype(kind)
                if count == 1:
                    out[part(f, many), :] = value
                    return
                for v in range(many // block):
                    row = ((f * (many // block) + v) * count + u) * block
                    here = pl.ds(pl.multiple_of(row, block), block)
                    out[here, :] = value[v * block : (v + 1) * block]

            loop(count * rows_of // many, tile_row)
            if kind == BF:
                total.core_send()

    def up_grad(total, count, which):
        ffn_grad(total, count, which, D, lambda p, f: ntb[:, f], lambda p, at: ghb[p, :, at])

    def down_grad(total, count, which):
        ffn_grad(total, count, which, F, lambda p, f: actb[p, :, f], lambda p, at: cotb[:, at])

    up_grad(sums.up, 1, lambda u: y)
    down_grad(sums.down, 1, lambda u: y)
    sums.up.step()
    sums.down.step()

    def feed_other(t):
        @pl.when(t == 0)
        def _():
            spread[0].send(3)
            spread[1].send(3)
            spread[0].arrive(3)
            spread[1].arrive(3)
            for u in range(1, M):
                bias_copy(u).wait_recv()

        feed(lax.rem(y + t + 1, M))

    loop(M - 1, feed_other)

    def steps(i, plan):
        for when, which in plan.items():

            @pl.when(i == when)
            def _():
                for total in which:
                    total.step()

    gmid, gmw, gatt, gmod = ref.gmid, ref.gmw, ref.cotn, ref.gmod
    row, lane = iota((8, D), 0), iota((8, D), 1) // head
    pick_one = jnp.where((row >= PAIRS) & (lane == 2 * (row - PAIRS)), 1.0, 0.0)
    pick_two = jnp.where((row >= PAIRS) & (lane == 2 * (row - PAIRS) + 1), 1.0, 0.0)
    m_send, m_pass, m_arrive, m_drain = halo(
        lambda k: gmw.at[pl.ds(2 * k, 2), pl.ds(G, G)],
        lambda slot, k: gmw.at[pl.ds(2 * k, 2), pl.ds(pl.multiple_of(slot * G, G), G)],
        ref.gmsem,
    )
    s_send, s_pass, s_arrive, s_drain = halo(
        lambda k: stw.at[1, pl.ds(2 * k, 2)],
        lambda slot, k: stw.at[slot, pl.ds(2 * k, 2)],
        ref.stsem,
    )

    def middle_back(c):
        at = part(c, half)
        grad = g2o[at, :]
        normed, inverse = layer_norm(mid[at, :])
        weighted = []
        for i in range(group):
            s = c * group + i
            lo, hi = i * G, (i + 1) * G
            scale = mods[pl.ds(s, 1), 2 * D : 3 * D]
            weighted.append(grad[lo:hi] * (1.0 + scale))
            gmod[pl.ds(s, 1), 2 * D : 3 * D] = jnp.sum(
                grad[lo:hi] * normed[lo:hi], axis=0, keepdims=True
            )
            gmod[pl.ds(s, 1), 3 * D : 4 * D] = jnp.sum(grad[lo:hi], axis=0, keepdims=True)
        weighted = jnp.concatenate(weighted, axis=0)
        middle = cotb[at, :].astype(F32) + norm_back(weighted, normed, inverse)
        gmid[at, :] = middle
        rounded = middle.astype(BF)
        gatt[at, :] = rounded
        mixture = dot(rounded, wo[...], NT).astype(BF)
        gmw[pl.ds(c * group, group), G : 2 * G, :] = mixture.reshape(group, G, D)
        product = mixture.astype(F32) * mixx[at, :]
        ones = dot(pick_one, product, NT, PRECISE)
        twos = dot(pick_two, product, NT, PRECISE)
        first_lanes = iota((8, 2 * G), 1) < G
        for g in range(group // 2):
            lo, hi = g * 2 * G, (g + 1) * 2 * G
            one, two = ones[:, lo:hi], twos[:, lo:hi]
            s = c * group + 2 * g
            stw[1, s] += jnp.where(first_lanes, one, pltpu.roll(two, G, 1))
            stw[1, s + 1] += jnp.where(first_lanes, pltpu.roll(one, G, 1), two)
        for k in range(2):
            m_send(2 * c + k)
            s_send(2 * c + k)

    loop(2, middle_back)

    def pass_on(k):
        m_pass(k)
        s_pass(k)

    sums.up.step()
    up_grad(sums.up2, M - 1, lambda u: lax.rem(y + u + 1, M))
    down_grad(sums.down2, M - 1, lambda u: lax.rem(y + u + 1, M))
    pass_on(0)
    sums.up2.step()
    weight_grad(sums.out, mixs[...], lambda at: gatt[:, at])
    sums.down.step()

    gqkv = ref.gqkv

    def query_back(s):
        at = pl.ds(pl.multiple_of(s * G, G), G)
        times = cnt[s]
        for p in range(PAIRS):
            lo, hi = p * pair, (p + 1) * pair
            grads = apart(gmw[s, G : 2 * G, lo:hi])
            gprob = dot(qkv[s, :, 2 * D + lo : 2 * D + hi], grads, NT)
            gscore = prob[s * PAIRS + p] * (gprob - stw[1, s, PAIRS + p : PAIRS + p + 1, :])
            weight = (times * gscore.astype(BF).astype(F32)).astype(BF)
            gquery = dot(weight, qkv[s, :, D + lo : D + hi], TN) * factor
            gqkv[at, lo : lo + head] = gquery[0:G, 0:head].astype(BF)
            gqkv[at, lo + head : hi] = gquery[G : 2 * G, head:pair].astype(BF)

    def query_pass(k):
        query_back(2 * k)
        query_back(2 * k + 1)

        @pl.when(k == 1)
        def _():
            pass_on(1)

        steps(k, {1: [sums.down2]})

    loop(4, query_pass)

    sums.out.step()
    pass_on(2)
    weight_grad(sums.query, n1s[...].reshape(rows, D), lambda at: gqkv[:, at])
    l_arrive(0)

    def count_back(s):
        shift = [2 * G, G, 0]
        block = jnp.concatenate(
            [lwt[b, s][:, 0:G].astype(F32) - float(shift[b]) for b in range(3)], axis=1
        ).astype(jnp.int32)
        key = iota((G, W), 0)
        total = jnp.zeros((G, W), F32)
        for j in range(near):
            total = total + jnp.where(block[j : j + 1, :] == key, 1.0, 0.0)
        cntt[s] = total

    loop(S, count_back)

    def finish_out(k):
        at = part(k)
        value = mid[at, :] + ref.bdn[...].astype(F32).reshape(1, D)
        for p in range(M):
            value = value + dot(actb[p, at, :], wdn[p])
        ref.n1n[at, :] = value.astype(BF)

    loop(4, finish_out)
    pass_on(3)
    sums.query.step()
    sums.up2.step()

    def key_back(s):
        at = pl.ds(pl.multiple_of(s * G, G), G)
        times = cntt[s]
        stats = [
            jnp.concatenate([stw[b, s][:, i * G : (i + 1) * G] for b in range(3)], axis=1)
            for i in range(2)
        ]
        for p in range(PAIRS):
            lo, hi = p * pair, (p + 1) * pair
            queries, grads = qkv[s, :, lo:hi], gmw[s, :, lo:hi]
            scores = dot(apart(qkv[s, G : 2 * G, D + lo : D + hi]), queries, NT) * factor
            gprob = dot(apart(qkv[s, G : 2 * G, 2 * D + lo : 2 * D + hi]), grads, NT)
            gscores, weights = [], []
            for i in range(2):
                rows_of = slice(i * G, (i + 1) * G)
                log, delta = stats[i][p : p + 1], stats[i][PAIRS + p : PAIRS + p + 1]
                probs = jnp.exp(jnp.where(times > 0.0, scores[rows_of] - log, MASKED))
                gscore = probs * (gprob[rows_of] - delta)
                gscores.append((times * gscore.astype(BF).astype(F32)).astype(BF))
                weights.append((times * probs.astype(BF).astype(F32)).astype(BF))
            gkey = dot(jnp.concatenate(gscores, axis=0), queries) * factor
            gvalue = dot(jnp.concatenate(weights, axis=0), grads)
            for i in range(2):
                cols = pl.ds(D + lo + i * head, head)
                gqkv[at, cols] = gkey[i * G : (i + 1) * G, i * head : (i + 1) * head].astype(BF)
                cols = pl.ds(2 * D + lo + i * head, head)
                gqkv[at, cols] = gvalue[i * G : (i + 1) * G, i * head : (i + 1) * head].astype(BF)

    def key_pass(k):
        m_arrive(k)
        s_arrive(k)
        key_back(2 * k)
        key_back(2 * k + 1)

    loop(4, key_pass)

    keys, values = gqkv.at[:, D : 2 * D], gqkv.at[:, 2 * D : 3 * D]
    weight_grad(sums.key, n1s[...].reshape(rows, D), lambda at: keys[:, at])
    weight_grad(sums.value, n1s[...].reshape(rows, D), lambda at: values[:, at])
    sums.down2.step()
    sums.out.step()
    sums.up2.step()
    sums.key.step()
    sums.value.step()

    gdbs = ref.gdbs
    out_rows = ref.outr

    def first_back(c):
        at = part(c, half)
        grad = dot(gqkv[at, :], wqkv[...], NT)
        normed, inverse = layer_norm(xs[at, :].astype(F32))
        weighted = []
        for i in range(group):
            s = c * group + i
            lo, hi = i * G, (i + 1) * G
            here = pl.ds(pl.multiple_of(s * G, G), G)
            gmod[pl.ds(s, 1), 0:D] = jnp.sum(grad[lo:hi] * normed[lo:hi], axis=0, keepdims=True)
            gmod[pl.ds(s, 1), D : 2 * D] = jnp.sum(grad[lo:hi], axis=0, keepdims=True)
            gdbs[pl.ds(s, 1), :] = jnp.sum(cotb[here, :].astype(F32), axis=0, keepdims=True)
            weighted.append(grad[lo:hi] * (1.0 + mods[pl.ds(s, 1), 0:D]))
        weighted = jnp.concatenate(weighted, axis=0)
        g2o[at, :] = gmid[at, :] + norm_back(weighted, normed, inverse)
        steps(c, {0: [sums.query], 1: [sums.down2]})

    loop(2, first_back)

    tail = ref.tail
    tail[...] = jnp.zeros_like(tail)
    for c in range(4 * D // tile):
        tail[c * S : (c + 1) * S, :] = gmod[:, c * tile : (c + 1) * tile]
    base = 4 * D // tile * S
    for c in range(D // tile):
        tail[base + c * S : base + (c + 1) * S, :] = gdbs[:, c * tile : (c + 1) * tile]
    base_up = base + D // tile * S
    for c in range(F // tile):
        for p in range(M):
            row = base_up + p * (F // tile) + c
            tail[row : row + 1, :] = bupg[p, 0:1, c * tile : (c + 1) * tile]
    sums.tail.cs[...] = tail[:, sums.tail.other]
    sums.tail.part[...] = tail[:, sums.tail.mine]
    sums.tail.core_send()
    sums.key.step()
    sums.value.step()
    sums.out.step()

    for c in range(D // 128):
        lo, hi = c * 128, (c + 1) * 128
        for s in range(S):
            ref.turn[c, pl.ds(s, G, stride=S), :] = g2o[s * G : (s + 1) * G, lo:hi]
        out_rows[:, lo:hi] = ref.turn[c]
    write(out_rows, ref.o_rows)

    sums.tail.step()
    sums.up.step(2)
    sums.query.step()

    def order_back(k):
        ref.outl[part(k), :] = dot(pt[part(k), :], ref.n1n[...]).astype(BF)

    loop(4, order_back)
    write(ref.outl, ref.o_layer)
    sums.down.step(2)
    sums.key.step()
    sums.value.step()
    sums.tail.step()
    sums.out.step(2)
    sums.up.step()
    sums.query.step(2)
    sums.value.step(2)
    sums.key.step(2)
    sums.down.step()
    sums.tail.step(2)
    sums.out.step()
    sums.query.step()
    sums.value.step()
    sums.key.step()
    sums.up.step()
    sums.tail.step()
    sums.out.step()
    sums.query.step()
    sums.value.step()
    sums.key.step()
    sums.down.step()
    sums.tail.step()
    late = (sums.up, sums.down, sums.query, sums.out, sums.key, sums.value, sums.tail)
    results = (ref.o_up, ref.o_dn, ref.o_q, ref.o_out, ref.o_k, ref.o_v, ref.o_tail)
    for total, result in zip(late, results):
        while total.todo:
            total.step()
        total.arrive()
        write(total.out, result)
    for total in (*late, sums.up2, sums.down2):
        total.finish()
    for c in written:
        c.wait()

    loop(4, x_drain)
    l_drain(0)
    loop(4, m_drain)
    loop(4, s_drain)

    for part_of in spread:
        part_of.drain()
    for t in range(1, M):
        bias_copy(t).wait_send()


WIDE = ("o_up", "o_dn", "o_out", "o_q", "o_k", "o_v")


def widen(static, names, *refs):
    ref = SimpleNamespace(**dict(zip(names, refs)))
    M, D, F, S = static
    tile = 256
    y = lax.axis_index("mlp")
    sources = (ref.o_up, ref.o_dn, ref.o_out, ref.o_q, ref.o_k, ref.o_v)
    targets = (
        ref.f_up,
        ref.f_dn,
        ref.f_out,
        ref.f_q,
        ref.f_kv.at[:, 0:D],
        ref.f_kv.at[:, D : 2 * D],
    )
    n = len(sources)
    tail_in = pltpu.make_async_copy(ref.o_tail, ref.tail, ref.isem.at[n])
    tail_in.start()
    loads = []
    for i, source in enumerate(sources):
        loads.append(pltpu.make_async_copy(source, ref.inb[i], ref.isem.at[i]))
        loads[-1].start()
    straight = [
        (ref.o_layer, ref.layer, ref.f_layer),
        (ref.o_rows, ref.rows, ref.f_rows),
    ]
    for i, (source, middle, _) in enumerate(straight):
        pltpu.make_async_copy(source, middle, ref.isem.at[n + 1 + i]).start()
    stores = []
    for i in range(n):
        loads[i].wait()
        count = sources[i].shape[0] // 128

        def part(k):
            at = pl.ds(pl.multiple_of(k * 128, 128), 128)
            ref.outb[i][at, :] = ref.inb[i][at, :].astype(F32)

        loop(count, part)
        stores.append(pltpu.make_async_copy(ref.outb[i], targets[i], ref.osem.at[i]))
        stores[-1].start()
    for i, (source, middle, target) in enumerate(straight):
        pltpu.make_async_copy(source, middle, ref.isem.at[n + 1 + i]).wait()
        stores.append(pltpu.make_async_copy(middle, target, ref.osem.at[n + 1 + i]))
        stores[-1].start()
    tail_in.wait()
    tail, gms = ref.tail, ref.gms
    pick = jnp.zeros((S, S), F32)
    for s in range(S):
        hit = (iota((S, S), 1) == s) & (iota((S, S), 0) == ref.sid[s])
        pick = pick + jnp.where(hit, 1.0, 0.0)
    for c in range(4 * D // tile):
        gms[:, c * tile : (c + 1) * tile] = dot(pick, tail[c * S : (c + 1) * S, :], NN, PRECISE)
    total = gms[...]
    ref.ada[...] = dot(ref.nc[...].astype(F32), total, TN, PRECISE)
    stores.append(pltpu.make_async_copy(ref.ada, ref.f_ada, ref.osem.at[n]))
    stores[-1].start()
    ref.f_adab[...] = jnp.sum(total, axis=0)
    ref.f_cond[...] = dot(total, ref.adaw[...].astype(F32), NT, PRECISE)
    base = 4 * D // tile * S
    for c in range(D // tile):
        ref.f_downb[c * tile : (c + 1) * tile] = jnp.sum(
            tail[base + c * S : base + (c + 1) * S, :], axis=0
        )
    base += D // tile * S
    for c in range(F // tile):
        row = tail[pl.ds(base + y * (F // tile) + c, 1), :]
        ref.f_upb[c * tile : (c + 1) * tile] = row.reshape(tile)
    for c in stores:
        c.wait()


def shards(
    node_rows,
    noise_cond,
    sample_id,
    neighbours,
    ada_weight,
    ada_bias,
    query_weight,
    keyval_weight,
    out_weight,
    up_weight,
    up_bias,
    down_weight,
    down_bias,
    cotangent,
):
    rows, D = node_rows.shape
    F = up_weight.shape[1]
    S, cond = noise_cond.shape
    near = neighbours.shape[1]
    R, M = lax.axis_size("rows"), lax.axis_size("mlp")
    nz = R // 4
    G = rows // S
    W = 3 * G
    small = 16 * nz if 16 * nz > 88 else 128
    V, H = pltpu.VMEM, pl.ANY
    shape = jax.ShapeDtypeStruct
    arguments = dict(
        x=(node_rows, H),
        nc=(noise_cond, V),
        sid=(sample_id, pltpu.SMEM),
        nbr=(neighbours.T, V),
        adaw=(ada_weight, V),
        adab=(ada_bias, V),
        wq=(query_weight, H),
        wkv=(keyval_weight, H),
        wo=(out_weight, H),
        wup=(up_weight, H),
        bup=(up_bias, V),
        wdn=(down_weight, H),
        bdn=(down_bias, V),
        cot=(cotangent, H),
    )
    outputs = dict(
        o_layer=shape((rows, D), BF),
        o_rows=shape((rows, D), F32),
        o_q=shape((D, D), BF),
        o_k=shape((D, D), BF),
        o_v=shape((D, D), BF),
        o_out=shape((D, D), BF),
        o_up=shape((D, F), BF),
        o_dn=shape((F, D), BF),
        o_tail=shape((small, 256), F32),
    )
    scratch = dict(
        xb=V((3, rows, D), BF),
        cotn=V((rows, D), BF),
        wqkv=V((D, 3 * D), BF),
        wob=V((D, D), BF),
        wupb=V((M, D, F), BF),
        wdnb=V((M, F, D), BF),
        pm=V((rows, rows), BF),
        pt=V((rows, rows), BF),
        lws=V((rows + G, near), F32),
        lwt=V((3, S, near, 2 * G), BF),
        mod=V((S, 4 * D), F32),
        mods=V((S, 4 * D), F32),
        n1n=V((rows, D), BF),
        n1s=V((S, G, D), BF),
        pq=V((rows // 4, rows // 4), BF),
        xs=V((rows, D), BF),
        qkv=V((S, W, 3 * D), BF),
        cotb=V((rows, D), BF),
        cnt=V((S, W, 2 * G), F32),
        cntt=V((S, G, W), F32),
        mixs=V((rows, D), BF),
        mixx=V((rows, D), F32),
        prob=V((S * PAIRS, W, 2 * G), F32),
        ntb=V((rows, D), BF),
        mid=V((rows, D), F32),
        actb=V((M, rows, F), BF),
        ghb=V((M, rows, F), BF),
        bupg=V((M, 8, F), F32),
        upb=V((M, 8, F), F32),
        g2o=V((rows, D), F32),
        gmid=V((rows, D), F32),
        gmw=V((S, W, D), BF),
        stw=V((3, S, 8, 2 * G), F32),
        gmod=V((S, 4 * D), F32),
        gqkv=V((rows, 3 * D), BF),
        gdbs=V((S, D), F32),
        turn=V((D // 128, rows, 128), F32),
        tail=V((small, 256), F32),
        outr=V((rows, D), F32),
        outl=V((rows, D), BF),
    )
    sums = []
    wide = ((D, F), (F, D), (D, F), (F, D), *[(D, D)] * 4, (small, 256))
    for i, (n, c) in enumerate(wide):
        dtype = F32 if i == len(SUMS) - 1 else BF
        times = M - 1 if ROLES[i] == OTHERS else 1
        stage = (n * times, c // 2)
        out = V((8, 128) if ROLES[i] == OTHERS else (n, c), dtype)
        bufs = [out, V(stage, F32)] + [V(stage, dtype)] * 3
        if ROLES[i] == OWN:
            bufs.append(V((M - 1, n // (2 * nz), c // 2), dtype))
        elif ROLES[i] == PLAIN and 0 not in sharing(i, n, M, nz):
            bufs.append(V((M, n // (2 * nz), c // 2), dtype))
        sums.append(tuple(bufs))
    scratch.update(sums=tuple(sums))
    sem = pltpu.SemaphoreType.DMA
    for name, dims in dict(
        xsem=(2, 4),
        spsem=(2 * (M - 1) * (nz + 2),),
        ubsem=(M - 1,),
        lwsem=(2, 1),
        gmsem=(2, 4),
        stsem=(2, 4),
        sumsem=(len(SUMS) * Sum.slots(nz, M),),
    ).items():
        scratch[name] = (sem(dims), sem(dims))
    scratch.update(lsem=sem((7,)), wsem=sem((len(outputs),)))
    names = [*arguments, *outputs, *scratch]
    results = pl.pallas_call(
        functools.partial(kernel, (R, M, rows, D, F, S, near), names),
        out_shape=[*outputs.values()],
        in_specs=[pl.BlockSpec(memory_space=m) for _, m in arguments.values()],
        out_specs=[pl.BlockSpec(memory_space=H) for _ in outputs],
        scratch_shapes=[*scratch.values()],
        name="layer",
        compiler_params=pltpu.CompilerParams(
            collective_id=0, has_side_effects=True, vmem_limit_bytes=63 * 2**20
        ),
    )(*[a for a, _ in arguments.values()])
    got = dict(zip(outputs, results))
    inputs = dict(
        nc=(noise_cond, V),
        sid=(sample_id, pltpu.SMEM),
        adaw=(ada_weight, V),
        **{name: (value, H) for name, value in got.items()},
    )
    finals = dict(
        f_layer=shape((rows, D), BF),
        f_rows=shape((rows, D), F32),
        f_cond=shape((S, cond), F32),
        f_ada=shape((cond, 4 * D), F32),
        f_adab=shape((4 * D,), F32),
        f_q=shape((D, D), F32),
        f_kv=shape((D, 2 * D), F32),
        f_out=shape((D, D), F32),
        f_up=shape((D, F), F32),
        f_upb=shape((F,), F32),
        f_dn=shape((F, D), F32),
        f_downb=shape((D,), F32),
    )
    small_ones = ("f_cond", "f_adab", "f_upb", "f_downb")
    room = dict(
        inb=tuple(V(got[name].shape, BF) for name in WIDE),
        outb=tuple(V(got[name].shape, F32) for name in WIDE),
        tail=V((small, 256), F32),
        ada=V((cond, 4 * D), F32),
        layer=V((rows, D), BF),
        rows=V((rows, D), F32),
        gms=V((S, 4 * D), F32),
        isem=sem((len(WIDE) + 3,)),
        osem=sem((len(WIDE) + 3,)),
    )
    return pl.pallas_call(
        functools.partial(widen, (M, D, F, S), [*inputs, *finals, *room]),
        out_shape=[*finals.values()],
        in_specs=[pl.BlockSpec(memory_space=m) for _, m in inputs.values()],
        out_specs=[
            pl.BlockSpec(memory_space=V if name in small_ones else H) for name in finals
        ],
        scratch_shapes=[*room.values()],
        name="widen",
        compiler_params=pltpu.CompilerParams(vmem_limit_bytes=62 * 2**20),
    )(*[a for a, _ in inputs.values()])


def solution(mesh):
    both = P(("rows", "mlp"), None)
    placed = (
        both,
        P(),
        P(("rows", "mlp")),
        both,
        P(),
        P(),
        P(),
        P(),
        P(),
        P(None, "mlp"),
        P("mlp"),
        P("mlp", None),
        P(),
        both,
    )
    return jax.shard_map(
        shards,
        mesh=mesh,
        in_specs=placed,
        out_specs=(
            both,
            both,
            P(),
            P(),
            P(),
            P(),
            P(),
            P(),
            P(None, "mlp"),
            P("mlp"),
            P("mlp", None),
            P(),
        ),
        check_vma=False,
    )
```

time: 174 us -> 140 us (0.80)
  Pallas kernels: 153 us -> 139 us
  local copies, waits for them, and re-layouts: 10.6 us -> 0 us
  other arithmetic: 9.21 us -> 0 us
    pallas_call x1, Pallas kernels: 153 us -> 130 us  [shards(): pl.pallas_call(functools.partial(kernel, (R, M, rows, D, F, S, near), nam...]
    convert_element_type x5 -> x0, other arithmetic: 9.21 us -> none  [the longest x1 2.23 us: shards(): got.o_q.astype(F32)]
    pallas_call x0 -> x1, Pallas kernels: none -> 8.2 us  [shards(): pl.pallas_call(functools.partial(widen, (M, D, F, S), [*inputs, *finals,...]
    unnamed x28 -> x0, local copies, waits for them, and re-layouts: 6.73 us -> none
    broadcast_in_dim x3 -> x0, local copies, waits for them, and re-layouts: 3.83 us -> none  [the longest x1 1.29 us: shards(): ada_bias[None]]
where the time goes in v2:
time: 140 us; the launch traced here: 139 us
  Pallas kernels  139 us (99%)
    pallas_call x1, Pallas kernels, shards(): pl.pallas_call(functools.partial(kernel, (R, M, rows, D, F, S, near), nam...  130 us
    pallas_call x1, Pallas kernels, shards(): pl.pallas_call(functools.partial(widen, (M, D, F, S), [*inputs, *finals,...  8.2 us

profile of v2, /device:TPU:0, one launch (start us, length us, event | category | flops | bytes accessed | tf_op | source)
XLA Modules:
  0.0 139.4 jit_solution(1693741352045711586)
XLA Ops:
  0.6 130.3 %layer.1 = (bf16[512,512]{1,0:T(8,128)(2,1)}, f32[512,512]{1,0:T(8,128)}, bf16[512,512]{1,0:T(8,128)(2,1)}, bf16[512,512]{1,0:T(8,128)(2,1)}, bf16[512,512]{1,0:...) custom-call(bf16[512,512]{1,0:T(8,128)(2,1)} %refs_0_.2, ...), custom_call_target="tpu_custom_call" | custom-call | tf_op jit(solution)/shard_map/layer/pallas_call | solution.py:1186
  131.0 8.2 %widen.1 = (bf16[512,512]{1,0:T(8,128)(2,1)}, f32[512,512]{1,0:T(8,128)}, f32[8,128]{1,0:T(8,128)}, f32[128,2048]{1,0:T(8,128)}, f32[2048]{0:T(1024)}, /*index=5...) custom-call(bf16[8,128]{1,0:T(8,128)(2,1)} %refs_0_.3, ...), custom_call_target="tpu_custom_call" | custom-call | tf_op jit(solution)/shard_map/widen/pallas_call | solution.py:1230

commit v3 on v2

--- a/solution.py
+++ b/solution.py
@@ -43,6 +43,10 @@
     return lax.broadcasted_iota(jnp.int32, shape, axis)
 
 
+def cut(start, size):
+    return pl.ds(start if isinstance(start, int) else pl.multiple_of(start, size), size)
+
+
 def loop(count, body):
     lax.fori_loop(0, count, lambda i, c: (body(i), c)[1], 0)
 
@@ -59,22 +63,28 @@
     )
 
 
+def sizes(m, nz):
+    return m, 2, nz, 2 * nz, 2, nz // 2
+
+
 class Sum:
     def __init__(self, out, dtype, bufs, sems, base, place, order, role):
         self.out, self.dtype, self.sems, self.base = out, dtype, sems, base
         self.part, self.cs, self.cr, self.rr = bufs[:4]
         self.place = place
         self.order = order
+        r, m, M, core, x, z, nz = place
+        self.index = (m, x, z, x * nz + z, lax.rem(z, 2), z // 2)
+        self.size = sizes(M, nz)
         self.role = role
+        self.shares = sum(self.size[axis] - 1 for axis in order)
+        self.last = self.shares if role == OTHERS else 2 * self.shares
         self.all_sum = role == PLAIN and 0 not in order
         self.back = order if role != OTHERS else ()
         self.mr = bufs[4] if len(bufs) > 4 else None
-        r, m, M, core, x, z, nz = place
-        self.index = (m, x, z, x * nz + z)
-        self.size = (M, 2, nz, 2 * nz)
         self.width = self.part.shape[1]
-        self.mine = pl.ds(pl.multiple_of(core * self.width, self.width), self.width)
-        self.other = pl.ds(pl.multiple_of((1 - core) * self.width, self.width), self.width)
+        self.mine = cut(core * self.width, self.width)
+        self.other = cut((1 - core) * self.width, self.width)
         self.start, self.length, self.stage = [0], [self.part.shape[0]], [0]
         for axis in order:
             length = self.length[-1] // self.size[axis]
@@ -108,12 +118,16 @@
             return z * 4 + (1 - x) * 2 + core, m
         if axis == 2:
             return lax.rem(z + t, nz) * 4 + x * 2 + core, m
+        if axis == 4:
+            return (z + 1 - 2 * lax.rem(z, 2)) * 4 + x * 2 + core, m
+        if axis == 5:
+            return lax.rem(z + 2 * t, nz) * 4 + x * 2 + core, m
         to = lax.rem(x * nz + z + t, 2 * nz)
         return lax.rem(to, nz) * 4 + to // nz * 2 + core, m
 
-    def slot(self, phase, axis, t):
-        M, _, nz, _ = self.size
-        return phase * (M + 3 * nz - 2) + (0, M - 1, M, M + nz - 1)[axis] + t - 1
+    def slot(self, phase, i, t):
+        before = sum(self.size[axis] - 1 for axis in self.order[:i])
+        return phase * self.shares + before + t - 1
 
     def copy(self, src, dst, slot, device):
         return remote(src, dst, self.sems, self.base + slot, device)
@@ -121,7 +135,7 @@
     def core_copy(self, phase):
         r, m, M, core, x, z, nz = self.place
         device = (z * 4 + x * 2 + 1 - core, m)
-        slot = 2 * (M + 3 * nz - 2) + phase
+        slot = self.last + phase
         if phase == 0:
             return self.copy(self.cs, self.cr, slot, device)
         block = self.out.at[:, self.mine]
@@ -131,21 +145,18 @@
         axis, length = self.order[i], self.length[i + 1]
         at = pl.ds(self.stage[i] + (t - 1) * length, length)
         return self.copy(
-            self.cs.at[at], self.rr.at[at], self.slot(0, axis, t), self.peer(axis, t)
+            self.cs.at[at], self.rr.at[at], self.slot(0, i, t), self.peer(axis, t)
         )
 
     def gather_copy(self, i, t):
         axis = self.back[i]
-        block = self.out.at[self.cut(self.begin[i + 1], self.extent[i + 1]), self.mine]
-        return self.copy(block, block, self.slot(1, axis, t), self.peer(axis, t))
+        block = self.out.at[cut(self.begin[i + 1], self.extent[i + 1]), self.mine]
+        return self.copy(block, block, self.slot(1, i, t), self.peer(axis, t))
 
     def mlp_copy(self, t):
         r, m, M, core, x, z, nz = self.place
         block = self.mr.at[m]
-        return self.copy(block, block, 2 * (M + 3 * nz - 2) + 1 + t, (r, lax.rem(m + t, M)))
-
-    def cut(self, start, size):
-        return pl.ds(pl.multiple_of(start, size), size)
+        return self.copy(block, block, self.last + 1 + t, (r, lax.rem(m + t, M)))
 
     def core_send(self):
         self.core_copy(0).start()
@@ -154,7 +165,7 @@
         if i == 0:
             self.core_copy(0).wait()
             return
-        at = self.cut(self.start[i], self.length[i])
+        at = cut(self.start[i], self.length[i])
         value = self.part[at, :]
         for t in range(1, self.size[self.order[i - 1]]):
             self.share_copy(i - 1, t).wait_recv()
@@ -169,7 +180,7 @@
         axis, length = self.order[i], self.length[i + 1]
         for t in range(1, self.size[axis]):
             block = lax.rem(self.index[axis] + t, self.size[axis])
-            at = self.cut(self.start[i] + block * length, length)
+            at = cut(self.start[i] + block * length, length)
             value = self.part[at, :]
             if i == 0:
                 value = value + self.cr[at, :].astype(F32)
@@ -180,7 +191,7 @@
         n = len(self.order)
         self.take(n)
         r, m, M, core, x, z, nz = self.place
-        self.mr[m] = self.part[self.cut(self.start[n], self.length[n]), :].astype(self.dtype)
+        self.mr[m] = self.part[cut(self.start[n], self.length[n]), :].astype(self.dtype)
         for t in range(1, M):
             self.mlp_copy(t).start()
 
@@ -188,20 +199,20 @@
         r, m, M, core, x, z, nz = self.place
         length = self.length[-1] // (M - 1)
         source = self.cs.at[pl.ds(self.stage[-1] + (t - 1) * length, length)]
-        slot = 2 * (M + 3 * nz - 2) + 1 + t
+        slot = self.last + t
         return self.copy(source, self.mate.mr.at[t - 1], slot, (r, lax.rem(m + t, M)))
 
     def send_over(self):
         n = len(self.order)
         self.take(n)
-        value = self.part[self.cut(self.start[n], self.length[n]), :]
+        value = self.part[cut(self.start[n], self.length[n]), :]
         self.cs[pl.ds(self.stage[n], self.length[n]), :] = value.astype(self.dtype)
         for t in range(1, self.size[0]):
             self.over_copy(t).start()
 
     def settle(self):
         n = len(self.order)
-        at = self.cut(self.start[n], self.length[n])
+        at = cut(self.start[n], self.length[n])
         if self.all_sum:
             for t in range(1, self.size[0]):
                 self.mlp_copy(t).wait_recv()
@@ -215,7 +226,7 @@
             for t in range(1, self.size[0]):
                 self.mate.over_copy(t).wait_recv()
                 value = value + self.mr[t - 1].astype(F32)
-        here = self.cut(self.begin[-1], self.extent[-1])
+        here = cut(self.begin[-1], self.extent[-1])
         self.out[here, self.mine] = value.astype(self.dtype)
 
     def gather(self, i):
@@ -251,55 +262,57 @@
                 self.mlp_copy(t).wait_send()
 
     @staticmethod
-    def slots(nz, m):
-        return 2 * (m + 3 * nz - 2) + 1 + m
+    def slots(order, role, nz, m):
+        shares = sum(sizes(m, nz)[axis] - 1 for axis in order)
+        if role == OTHERS:
+            return shares + m
+        return 2 * shares + 2 + (m - 1 if role == PLAIN and 0 not in order else 0)
 
 
 class Spread:
-    def __init__(self, source, parts, sems, base, place, z_first):
+    def __init__(self, source, parts, sems, base, place, sliced):
         self.source, self.parts, self.sems, self.base = source, parts, sems, base
-        self.z_first = z_first
-        self.place = place
+        self.place, self.sliced = place, sliced
         r, m, M, core, x, z, nz = place
         _, rows, cols = parts.shape
-        self.rows, self.piece, width = rows, rows // (2 * nz), cols // 2
+        self.rows, width = rows, cols // 2
         self.mine = pl.ds(pl.multiple_of(core * width, width), width)
-        self.here = self.cut((x * nz + z if z_first else z * 2 + x) * self.piece, self.piece)
-
-    def cut(self, start, size):
-        return pl.ds(pl.multiple_of(start, size), size)
+        piece = rows // (2 * nz)
+        self.here = cut((x * nz + z) * piece, piece) if sliced else pl.ds(0, rows)
+        self.each_peer = nz + 2 if sliced else 2
 
     def copies(self, stage, t):
         r, m, M, core, x, z, nz = self.place
-        base = self.base + (t - 1) * (nz + 2)
+        base = self.base + (t - 1) * self.each_peer
         if stage == 0:
             source = self.source.at[self.here, self.mine]
             target = self.parts.at[m, self.here, self.mine]
             return [remote(source, target, self.sems, base, (r, lax.rem(m + t, M)))]
         part = self.parts.at[lax.rem(m + M - t, M)]
-        over_z = [lax.rem(z + u, nz) * 4 + x * 2 + core for u in range(1, nz)]
-        over_x = [z * 4 + (1 - x) * 2 + core]
         if stage == 1:
             block = part.at[self.here, self.mine]
-            rows = over_z if self.z_first else over_x
+            rows = [lax.rem(z + u, nz) * 4 + x * 2 + core for u in range(1, nz)]
         elif stage == 2:
-            many = (nz if self.z_first else 2) * self.piece
-            block = part.at[self.cut((x if self.z_first else z) * many, many), self.mine]
-            rows = over_x if self.z_first else over_z
+            block = part.at[cut(x * (self.rows // 2), self.rows // 2), self.mine]
+            rows = [z * 4 + (1 - x) * 2 + core]
         else:
             block = part.at[:, self.mine]
             rows = [z * 4 + x * 2 + 1 - core]
-        first = base + (0, 1, nz if self.z_first else 2, nz + 1)[stage]
+        first = base + ((0, 1, nz, nz + 1)[stage] if self.sliced else 1)
         return [
             remote(block, block, self.sems, first + i, (row, m)) for i, row in enumerate(rows)
         ]
 
+    def stages(self):
+        return (0, 1, 2, 3) if self.sliced else (0, 3)
+
     def each(self, stage):
         return [c for t in range(1, self.place[2]) for c in self.copies(stage, t)]
 
     def send(self, stage):
-        if stage > 0:
-            self.arrive(stage - 1)
+        before = [i for i in self.stages() if i < stage]
+        if before:
+            self.arrive(before[-1])
         for c in self.each(stage):
             c.start()
 
@@ -308,7 +321,7 @@
             c.wait_recv()
 
     def drain(self):
-        for stage in range(4):
+        for stage in self.stages():
             for c in self.each(stage):
                 c.wait_send()
 
@@ -316,8 +329,8 @@
 PLAIN, OWN, OTHERS = 0, 1, 2
 SUMS = ("up", "down", "up2", "down2", "out", "query", "key", "value", "tail")
 ROLES = (OWN, OWN, OTHERS, OTHERS, PLAIN, PLAIN, PLAIN, PLAIN, PLAIN)
-FLAT, ALL = (1, 2), (0, 1, 2)
-ORDERS = (FLAT, FLAT, FLAT, FLAT, ALL, ALL, ALL, (1, 2, 0), (0, 3))
+FLAT = (1, 4, 5)
+ORDERS = (FLAT, FLAT, FLAT, FLAT, (0, 1, 2), (0, 1, 2), (0, 1, 2), (0, 1, 2), (0, 3))
 
 
 def sharing(i, rows, M, nz):
@@ -412,7 +425,7 @@
     quarter = rows // 4
 
     def part(k, n=quarter):
-        return pl.ds(pl.multiple_of(k * n, n), n)
+        return cut(k * n, n)
 
     x_send, x_pass, x_arrive, x_drain = halo(
         lambda k: ref.x.at[part(k)], lambda slot, k: xb.at[slot, part(k)], ref.xsem
@@ -473,7 +486,7 @@
     for s in range(S):
         mods[s : s + 1, :] = ref.mod[pl.ds(ref.sid[s], 1), :]
 
-    n1s, qkv = ref.n1s, ref.qkv
+    n1w, qkv = ref.n1w, ref.qkv
     wqkv = ref.wqkv
 
     turn16 = quarter // S
@@ -485,18 +498,15 @@
         scaled = scaled + mods[:, D : 2 * D][None]
         ordered = dot(ref.pq[...], scaled.reshape(quarter, D).astype(BF)).astype(BF)
         wide = dot(ordered, wqkv[...]).astype(BF).reshape(S, turn16, 3 * D)
-        here = pl.ds(pl.multiple_of(slot * G + k * turn16, turn16), turn16)
+        here = cut(slot * G + k * turn16, turn16)
         qkv[:, here, :] = wide
-        return ordered.reshape(S, turn16, D)
+        n1w[:, here, :] = ordered.reshape(S, turn16, D)
 
     local[0].wait()
     local[1].wait()
     local[2].wait()
 
-    def own_norm(k):
-        n1s[:, pl.ds(pl.multiple_of(k * turn16, turn16), turn16), :] = norm_block(1, k)
-
-    loop(4, own_norm)
+    loop(4, lambda k: norm_block(1, k))
     local[3].wait()
     xs, cotb = ref.xs, ref.cotb
 
@@ -530,10 +540,9 @@
         x_arrive(k)
         norm_block(far_slot, k)
 
-        @pl.when(k == 2)
+        @pl.when(k == 1)
         def _():
             spread[0].send(1)
-            spread[1].send(1)
 
     loop(4, far_norm)
 
@@ -550,7 +559,7 @@
     def attend(k):
         for s2 in range(2):
             s = 2 * k + s2
-            at = pl.ds(pl.multiple_of(s * G, G), G)
+            at = cut(s * G, G)
             times = cnt[s]
             logs = []
             for p in range(PAIRS):
@@ -592,16 +601,14 @@
             lo = i * G
             scale = mods[pl.ds(c * group + i, 1), 2 * D : 3 * D]
             shift = mods[pl.ds(c * group + i, 1), 3 * D : 4 * D]
-            here = pl.ds(pl.multiple_of(c * half + lo, G), G)
+            here = cut(c * half + lo, G)
             ntb[here, :] = (normed[lo : lo + G] * (1.0 + scale) + shift).astype(BF)
 
     loop(2, mix_out)
 
     local[5].wait()
     local[6].wait()
-    l_pass(0)
     spread[0].send(2)
-    spread[1].send(2)
     wup, wdn, actb, ghb = ref.wupb, ref.wdnb, ref.actb, ref.ghb
     bupg, g2o = ref.bupg, ref.g2o
     bupg[...] = jnp.zeros_like(bupg)
@@ -627,7 +634,7 @@
 
     feed(y)
 
-    count_of = Sum.slots(nz, M)
+    base = 0
     sums = SimpleNamespace()
     written = []
 
@@ -640,7 +647,8 @@
         out, *bufs = bufs
         dtype = F32 if i == len(SUMS) - 1 else BF
         order = sharing(i, bufs[0].shape[0], M, nz)
-        total = Sum(out, dtype, bufs, ref.sumsem, i * count_of, place_of, order, ROLES[i])
+        total = Sum(out, dtype, bufs, ref.sumsem, base, place_of, order, ROLES[i])
+        base += Sum.slots(order, ROLES[i], nz, M)
         setattr(sums, name, total)
     sums.up.mate, sums.down.mate, sums.up2.mate, sums.down2.mate = (
         sums.up2,
@@ -655,7 +663,7 @@
             (total.cs, (1 - core) * width, BF),
             (total.part, core * width, F32),
         ):
-            at = pl.ds(pl.multiple_of(start, width), width)
+            at = cut(start, width)
             out[...] = dot(left, right(at), TN).astype(kind)
             if kind == BF:
                 total.core_send()
@@ -667,7 +675,7 @@
             (total.cs, (1 - core) * width, BF),
             (total.part, core * width, F32),
         ):
-            at = pl.ds(pl.multiple_of(start, width), width)
+            at = cut(start, width)
 
             def tile_row(i):
                 u, f = i // (rows_of // many), lax.rem(i, rows_of // many)
@@ -678,7 +686,7 @@
                     return
                 for v in range(many // block):
                     row = ((f * (many // block) + v) * count + u) * block
-                    here = pl.ds(pl.multiple_of(row, block), block)
+                    here = cut(row, block)
                     out[here, :] = value[v * block : (v + 1) * block]
 
             loop(count * rows_of // many, tile_row)
@@ -691,6 +699,7 @@
     def down_grad(total, count, which):
         ffn_grad(total, count, which, F, lambda p, f: actb[p, :, f], lambda p, at: cotb[:, at])
 
+    l_pass(0)
     up_grad(sums.up, 1, lambda u: y)
     down_grad(sums.down, 1, lambda u: y)
     sums.up.step()
@@ -710,21 +719,13 @@
 
     loop(M - 1, feed_other)
 
-    def steps(i, plan):
-        for when, which in plan.items():
-
-            @pl.when(i == when)
-            def _():
-                for total in which:
-                    total.step()
-
     gmid, gmw, gatt, gmod = ref.gmid, ref.gmw, ref.cotn, ref.gmod
     row, lane = iota((8, D), 0), iota((8, D), 1) // head
     pick_one = jnp.where((row >= PAIRS) & (lane == 2 * (row - PAIRS)), 1.0, 0.0)
     pick_two = jnp.where((row >= PAIRS) & (lane == 2 * (row - PAIRS) + 1), 1.0, 0.0)
     m_send, m_pass, m_arrive, m_drain = halo(
         lambda k: gmw.at[pl.ds(2 * k, 2), pl.ds(G, G)],
-        lambda slot, k: gmw.at[pl.ds(2 * k, 2), pl.ds(pl.multiple_of(slot * G, G), G)],
+        lambda slot, k: gmw.at[pl.ds(2 * k, 2), cut(slot * G, G)],
         ref.gmsem,
     )
     s_send, s_pass, s_arrive, s_drain = halo(
@@ -768,24 +769,17 @@
             m_send(2 * c + k)
             s_send(2 * c + k)
 
-    loop(2, middle_back)
-
     def pass_on(k):
         m_pass(k)
         s_pass(k)
 
-    sums.up.step()
-    up_grad(sums.up2, M - 1, lambda u: lax.rem(y + u + 1, M))
-    down_grad(sums.down2, M - 1, lambda u: lax.rem(y + u + 1, M))
-    pass_on(0)
-    sums.up2.step()
-    weight_grad(sums.out, mixs[...], lambda at: gatt[:, at])
-    sums.down.step()
-
-    gqkv = ref.gqkv
+    def other_part(u):
+        return lax.rem(y + u + 1, M)
+
+    gqkv, gkvw = ref.gqkv, ref.gkvw
 
     def query_back(s):
-        at = pl.ds(pl.multiple_of(s * G, G), G)
+        at = cut(s * G, G)
         times = cnt[s]
         for p in range(PAIRS):
             lo, hi = p * pair, (p + 1) * pair
@@ -796,23 +790,11 @@
             gquery = dot(weight, qkv[s, :, D + lo : D + hi], TN) * factor
             gqkv[at, lo : lo + head] = gquery[0:G, 0:head].astype(BF)
             gqkv[at, lo + head : hi] = gquery[G : 2 * G, head:pair].astype(BF)
-
-    def query_pass(k):
-        query_back(2 * k)
-        query_back(2 * k + 1)
-
-        @pl.when(k == 1)
-        def _():
-            pass_on(1)
-
-        steps(k, {1: [sums.down2]})
-
-    loop(4, query_pass)
-
-    sums.out.step()
-    pass_on(2)
-    weight_grad(sums.query, n1s[...].reshape(rows, D), lambda at: gqkv[:, at])
-    l_arrive(0)
+            queries = apart(qkv[s, G : 2 * G, lo:hi])
+            gkvw[s, :, lo:hi] = (dot(weight, queries) * factor).astype(BF)
+            weight = (times * prob[s * PAIRS + p].astype(BF).astype(F32)).astype(BF)
+            gkvw[s, :, D + lo : D + hi] = dot(weight, grads).astype(BF)
+
 
     def count_back(s):
         shift = [2 * G, G, 0]
@@ -825,8 +807,6 @@
             total = total + jnp.where(block[j : j + 1, :] == key, 1.0, 0.0)
         cntt[s] = total
 
-    loop(S, count_back)
-
     def finish_out(k):
         at = part(k)
         value = mid[at, :] + ref.bdn[...].astype(F32).reshape(1, D)
@@ -834,13 +814,9 @@
             value = value + dot(actb[p, at, :], wdn[p])
         ref.n1n[at, :] = value.astype(BF)
 
-    loop(4, finish_out)
-    pass_on(3)
-    sums.query.step()
-    sums.up2.step()
 
     def key_back(s):
-        at = pl.ds(pl.multiple_of(s * G, G), G)
+        at = cut(s * G, G)
         times = cntt[s]
         stats = [
             jnp.concatenate([stw[b, s][:, i * G : (i + 1) * G] for b in range(3)], axis=1)
@@ -867,22 +843,6 @@
                 cols = pl.ds(2 * D + lo + i * head, head)
                 gqkv[at, cols] = gvalue[i * G : (i + 1) * G, i * head : (i + 1) * head].astype(BF)
 
-    def key_pass(k):
-        m_arrive(k)
-        s_arrive(k)
-        key_back(2 * k)
-        key_back(2 * k + 1)
-
-    loop(4, key_pass)
-
-    keys, values = gqkv.at[:, D : 2 * D], gqkv.at[:, 2 * D : 3 * D]
-    weight_grad(sums.key, n1s[...].reshape(rows, D), lambda at: keys[:, at])
-    weight_grad(sums.value, n1s[...].reshape(rows, D), lambda at: values[:, at])
-    sums.down2.step()
-    sums.out.step()
-    sums.up2.step()
-    sums.key.step()
-    sums.value.step()
 
     gdbs = ref.gdbs
     out_rows = ref.outr
@@ -895,96 +855,187 @@
         for i in range(group):
             s = c * group + i
             lo, hi = i * G, (i + 1) * G
-            here = pl.ds(pl.multiple_of(s * G, G), G)
+            here = cut(s * G, G)
             gmod[pl.ds(s, 1), 0:D] = jnp.sum(grad[lo:hi] * normed[lo:hi], axis=0, keepdims=True)
             gmod[pl.ds(s, 1), D : 2 * D] = jnp.sum(grad[lo:hi], axis=0, keepdims=True)
             gdbs[pl.ds(s, 1), :] = jnp.sum(cotb[here, :].astype(F32), axis=0, keepdims=True)
             weighted.append(grad[lo:hi] * (1.0 + mods[pl.ds(s, 1), 0:D]))
         weighted = jnp.concatenate(weighted, axis=0)
         g2o[at, :] = gmid[at, :] + norm_back(weighted, normed, inverse)
-        steps(c, {0: [sums.query], 1: [sums.down2]})
-
-    loop(2, first_back)
 
     tail = ref.tail
-    tail[...] = jnp.zeros_like(tail)
-    for c in range(4 * D // tile):
-        tail[c * S : (c + 1) * S, :] = gmod[:, c * tile : (c + 1) * tile]
     base = 4 * D // tile * S
-    for c in range(D // tile):
-        tail[base + c * S : base + (c + 1) * S, :] = gdbs[:, c * tile : (c + 1) * tile]
     base_up = base + D // tile * S
-    for c in range(F // tile):
-        for p in range(M):
-            row = base_up + p * (F // tile) + c
-            tail[row : row + 1, :] = bupg[p, 0:1, c * tile : (c + 1) * tile]
-    sums.tail.cs[...] = tail[:, sums.tail.other]
-    sums.tail.part[...] = tail[:, sums.tail.mine]
-    sums.tail.core_send()
-    sums.key.step()
-    sums.value.step()
-    sums.out.step()
-
-    for c in range(D // 128):
-        lo, hi = c * 128, (c + 1) * 128
-        for s in range(S):
-            ref.turn[c, pl.ds(s, G, stride=S), :] = g2o[s * G : (s + 1) * G, lo:hi]
-        out_rows[:, lo:hi] = ref.turn[c]
-    write(out_rows, ref.o_rows)
-
-    sums.tail.step()
-    sums.up.step(2)
-    sums.query.step()
+
+    def pack_tail():
+        tail[...] = jnp.zeros_like(tail)
+        for c in range(4 * D // tile):
+            tail[c * S : (c + 1) * S, :] = gmod[:, c * tile : (c + 1) * tile]
+        for c in range(D // tile):
+            tail[base + c * S : base + (c + 1) * S, :] = gdbs[:, c * tile : (c + 1) * tile]
+        for c in range(F // tile):
+            for p in range(M):
+                row = base_up + p * (F // tile) + c
+                tail[row : row + 1, :] = bupg[p, 0:1, c * tile : (c + 1) * tile]
+        sums.tail.cs[...] = tail[:, sums.tail.other]
+        sums.tail.part[...] = tail[:, sums.tail.mine]
+        sums.tail.core_send()
+
+    def rows_back():
+        for c in range(D // 128):
+            lo, hi = c * 128, (c + 1) * 128
+            for s in range(S):
+                ref.turn[c, pl.ds(s, G, stride=S), :] = g2o[s * G : (s + 1) * G, lo:hi]
+            out_rows[:, lo:hi] = ref.turn[c]
+        write(out_rows, ref.o_rows)
 
     def order_back(k):
         ref.outl[part(k), :] = dot(pt[part(k), :], ref.n1n[...]).astype(BF)
 
-    loop(4, order_back)
-    write(ref.outl, ref.o_layer)
+
+    def drain():
+        loop(4, x_drain)
+        l_drain(0)
+        loop(4, m_drain)
+        loop(4, s_drain)
+        for part_of in spread:
+            part_of.drain()
+        for t in range(1, M):
+            bias_copy(t).wait_send()
+        sums.up2.finish()
+        sums.down2.finish()
+
+    def out_grad():
+        weight_grad(sums.out, mixs[...], lambda at: gatt[:, at])
+
+    def query_grad():
+        weight_grad(sums.query, n1w[:, G : 2 * G, :].reshape(rows, D), lambda at: gqkv[:, at])
+
+    def window_grad(total, shares):
+        left = n1w[...].reshape(S * W, D)
+        weight_grad(total, left, lambda at: shares[:, :, at].reshape(S * W, at.size))
+
+    def key_grad():
+        window_grad(sums.key, gkvw.at[:, :, 0:D])
+
+    def value_grad():
+        window_grad(sums.value, gkvw.at[:, :, D : 2 * D])
+
+    def queries_of(k):
+        query_back(2 * k)
+        query_back(2 * k + 1)
+
+    def keys_of(k):
+        m_arrive(k)
+        s_arrive(k)
+        key_back(2 * k)
+        key_back(2 * k + 1)
+
+    def counts():
+        l_arrive(0)
+        loop(S, count_back)
+
+    def layer_out():
+        loop(4, finish_out)
+
+    def layer_order():
+        loop(4, order_back)
+        write(ref.outl, ref.o_layer)
+
+    sums.up.step()
+    up_grad(sums.up2, M - 1, other_part)
+    down_grad(sums.down2, M - 1, other_part)
+    sums.up2.step()
+    middle_back(0)
+    sums.up.step()
+    sums.down.step()
+    sums.down2.step()
+    middle_back(1)
+    out_grad()
+    sums.out.step()
+    queries_of(0)
+    sums.down.step()
+    queries_of(1)
+    sums.up2.step()
+    queries_of(2)
+    queries_of(3)
+    pass_on(0)
+    pass_on(1)
+    query_grad()
+    sums.query.step()
+    sums.up2.step()
+    key_grad()
+    sums.key.step()
+    pass_on(2)
+    sums.down2.step()
+    value_grad()
+    sums.value.step()
+    pass_on(3)
+    counts()
+    sums.down2.step()
+    layer_out()
+    sums.out.step()
+    sums.up2.step()
+    keys_of(0)
+    keys_of(1)
+    sums.query.step()
+    keys_of(2)
+    keys_of(3)
+    sums.out.step()
+    sums.key.step()
+    first_back(0)
+    sums.query.step()
+    sums.down2.step()
+    first_back(1)
+    pack_tail()
+    sums.up.step(2)
+    sums.value.step()
+    rows_back()
+    layer_order()
+    sums.tail.step()
+    sums.key.step()
+    sums.out.step(2)
+    sums.query.step(2)
+    sums.value.step()
+    sums.key.step(2)
+    sums.tail.step()
     sums.down.step(2)
-    sums.key.step()
-    sums.value.step()
-    sums.tail.step()
-    sums.out.step(2)
     sums.up.step()
-    sums.query.step(2)
-    sums.value.step(2)
-    sums.key.step(2)
-    sums.down.step()
-    sums.tail.step(2)
     sums.out.step()
     sums.query.step()
     sums.value.step()
+    sums.tail.step()
+    sums.value.step()
+    sums.up.step()
     sums.key.step()
+    sums.out.step()
+    sums.tail.step()
+    sums.query.step()
+    sums.down.step()
+    sums.value.step()
     sums.up.step()
+    sums.key.step()
+    sums.out.step()
     sums.tail.step()
-    sums.out.step()
     sums.query.step()
     sums.value.step()
+    sums.down.step()
     sums.key.step()
+    drain()
+    sums.value.step()
+    sums.tail.step()
     sums.down.step()
-    sums.tail.step()
-    late = (sums.up, sums.down, sums.query, sums.out, sums.key, sums.value, sums.tail)
-    results = (ref.o_up, ref.o_dn, ref.o_q, ref.o_out, ref.o_k, ref.o_v, ref.o_tail)
+    late = (sums.up, sums.out, sums.query, sums.key, sums.value, sums.tail, sums.down)
+    results = (ref.o_up, ref.o_out, ref.o_q, ref.o_k, ref.o_v, ref.o_tail, ref.o_dn)
     for total, result in zip(late, results):
         while total.todo:
             total.step()
         total.arrive()
         write(total.out, result)
-    for total in (*late, sums.up2, sums.down2):
+    for total in late:
         total.finish()
     for c in written:
         c.wait()
-
-    loop(4, x_drain)
-    l_drain(0)
-    loop(4, m_drain)
-    loop(4, s_drain)
-
-    for part_of in spread:
-        part_of.drain()
-    for t in range(1, M):
-        bias_copy(t).wait_send()
 
 
 WIDE = ("o_up", "o_dn", "o_out", "o_q", "o_k", "o_v")
@@ -1005,34 +1056,45 @@
         ref.f_kv.at[:, D : 2 * D],
     )
     n = len(sources)
+    straight = ((ref.o_rows, ref.rows, ref.f_rows), (ref.o_layer, ref.layer, ref.f_layer))
+    passing = []
+    for i, (source, middle, target) in enumerate(straight):
+        load = pltpu.make_async_copy(source, middle, ref.isem.at[n + 1 + i])
+        passing.append((load, pltpu.make_async_copy(middle, target, ref.osem.at[n + 1 + i])))
+        load.start()
+    loads = [
+        pltpu.make_async_copy(source, ref.inb[i], ref.isem.at[i])
+        for i, source in enumerate(sources)
+    ]
     tail_in = pltpu.make_async_copy(ref.o_tail, ref.tail, ref.isem.at[n])
+    loads[0].start()
+    loads[1].start()
     tail_in.start()
-    loads = []
-    for i, source in enumerate(sources):
-        loads.append(pltpu.make_async_copy(source, ref.inb[i], ref.isem.at[i]))
-        loads[-1].start()
-    straight = [
-        (ref.o_layer, ref.layer, ref.f_layer),
-        (ref.o_rows, ref.rows, ref.f_rows),
-    ]
-    for i, (source, middle, _) in enumerate(straight):
-        pltpu.make_async_copy(source, middle, ref.isem.at[n + 1 + i]).start()
+    for load in loads[2:]:
+        load.start()
     stores = []
-    for i in range(n):
+
+    def store(copy):
+        copy.start()
+        stores.append(copy)
+
+    for load, out in passing:
+        load.wait()
+        store(out)
+
+    def convert(i):
         loads[i].wait()
-        count = sources[i].shape[0] // 128
+        at_once = 128
 
         def part(k):
-            at = pl.ds(pl.multiple_of(k * 128, 128), 128)
+            at = cut(k * at_once, at_once)
             ref.outb[i][at, :] = ref.inb[i][at, :].astype(F32)
 
-        loop(count, part)
-        stores.append(pltpu.make_async_copy(ref.outb[i], targets[i], ref.osem.at[i]))
-        stores[-1].start()
-    for i, (source, middle, target) in enumerate(straight):
-        pltpu.make_async_copy(source, middle, ref.isem.at[n + 1 + i]).wait()
-        stores.append(pltpu.make_async_copy(middle, target, ref.osem.at[n + 1 + i]))
-        stores[-1].start()
+        loop(sources[i].shape[0] // at_once, part)
+        store(pltpu.make_async_copy(ref.outb[i], targets[i], ref.osem.at[i]))
+
+    convert(0)
+    convert(1)
     tail_in.wait()
     tail, gms = ref.tail, ref.gms
     pick = jnp.zeros((S, S), F32)
@@ -1043,8 +1105,9 @@
         gms[:, c * tile : (c + 1) * tile] = dot(pick, tail[c * S : (c + 1) * S, :], NN, PRECISE)
     total = gms[...]
     ref.ada[...] = dot(ref.nc[...].astype(F32), total, TN, PRECISE)
-    stores.append(pltpu.make_async_copy(ref.ada, ref.f_ada, ref.osem.at[n]))
-    stores[-1].start()
+    store(pltpu.make_async_copy(ref.ada, ref.f_ada, ref.osem.at[n]))
+    for i in range(2, n):
+        convert(i)
     ref.f_adab[...] = jnp.sum(total, axis=0)
     ref.f_cond[...] = dot(total, ref.adaw[...].astype(F32), NT, PRECISE)
     base = 4 * D // tile * S
@@ -1128,7 +1191,8 @@
         mod=V((S, 4 * D), F32),
         mods=V((S, 4 * D), F32),
         n1n=V((rows, D), BF),
-        n1s=V((S, G, D), BF),
+        n1w=V((S, W, D), BF),
+        gkvw=V((S, W, 2 * D), BF),
         pq=V((rows // 4, rows // 4), BF),
         xs=V((rows, D), BF),
         qkv=V((S, W, 3 * D), BF),
@@ -1158,10 +1222,12 @@
     )
     sums = []
     wide = ((D, F), (F, D), (D, F), (F, D), *[(D, D)] * 4, (small, 256))
+    count = 0
     for i, (n, c) in enumerate(wide):
         dtype = F32 if i == len(SUMS) - 1 else BF
         times = M - 1 if ROLES[i] == OTHERS else 1
         stage = (n * times, c // 2)
+        count += Sum.slots(sharing(i, n * times, M, nz), ROLES[i], nz, M)
         out = V((8, 128) if ROLES[i] == OTHERS else (n, c), dtype)
         bufs = [out, V(stage, F32)] + [V(stage, dtype)] * 3
         if ROLES[i] == OWN:
@@ -1178,7 +1244,7 @@
         lwsem=(2, 1),
         gmsem=(2, 4),
         stsem=(2, 4),
-        sumsem=(len(SUMS) * Sum.slots(nz, M),),
+        sumsem=(count,),
     ).items():
         scratch[name] = (sem(dims), sem(dims))
     scratch.update(lsem=sem((7,)), wsem=sem((len(outputs),)))

time: 140 us -> 126 us (0.900)
  Pallas kernels: 139 us -> 124 us
    pallas_call x1, Pallas kernels: 130 us -> 116 us  [shards(): pl.pallas_call(functools.partial(kernel, (R, M, rows, D, F, S, near), nam...]
where the time goes in v3:
time: 126 us; the launch traced here: 125 us
  Pallas kernels  124 us (98%)
    pallas_call x1, Pallas kernels, shards(): pl.pallas_call(functools.partial(kernel, (R, M, rows, D, F, S, near), nam...  116 us
    pallas_call x1, Pallas kernels, shards(): pl.pallas_call(functools.partial(widen, (M, D, F, S), [*inputs, *finals,...  8.24 us

profile of v3, /device:TPU:0, one launch (start us, length us, event | category | flops | bytes accessed | tf_op | source)
XLA Modules:
  0.0 124.8 jit_solution(6238653638939986750)
XLA Ops:
  0.6 115.7 %layer.1 = (bf16[512,512]{1,0:T(8,128)(2,1)}, f32[512,512]{1,0:T(8,128)}, bf16[512,512]{1,0:T(8,128)(2,1)}, bf16[512,512]{1,0:T(8,128)(2,1)}, bf16[512,512]{1,0:...) custom-call(bf16[512,512]{1,0:T(8,128)(2,1)} %refs_0_.2, ...), custom_call_target="tpu_custom_call" | custom-call | tf_op jit(solution)/shard_map/layer/pallas_call | solution.py:1252
  116.3 8.2 %widen.1 = (bf16[512,512]{1,0:T(8,128)(2,1)}, f32[512,512]{1,0:T(8,128)}, f32[8,128]{1,0:T(8,128)}, f32[128,2048]{1,0:T(8,128)}, f32[2048]{0:T(1024)}, /*index=5...) custom-call(bf16[8,128]{1,0:T(8,128)(2,1)} %refs_0_.3, ...), custom_call_target="tpu_custom_call" | custom-call | tf_op jit(solution)/shard_map/widen/pallas_call | solution.py:1296

commit v4 on v3

--- a/solution.py
+++ b/solution.py
@@ -244,8 +244,7 @@
     def arrive(self):
         self.core_copy(1).wait_recv()
 
-    def finish(self):
-        assert not self.todo
+    def release(self):
         for i, axis in enumerate(self.order):
             for t in range(1, self.size[axis]):
                 self.share_copy(i, t).wait_send()
@@ -253,13 +252,16 @@
             for t in range(1, self.size[0]):
                 self.over_copy(t).wait_send()
             return
-        self.core_copy(1).wait_send()
         for i, axis in enumerate(self.back):
             for t in range(1, self.size[axis]):
                 self.gather_copy(i, t).wait_send()
         if self.all_sum:
             for t in range(1, self.size[0]):
                 self.mlp_copy(t).wait_send()
+
+    def finish(self):
+        assert not self.todo
+        self.core_copy(1).wait_send()
 
     @staticmethod
     def slots(order, role, nz, m):
@@ -902,8 +904,12 @@
             part_of.drain()
         for t in range(1, M):
             bias_copy(t).wait_send()
-        sums.up2.finish()
-        sums.down2.finish()
+        sums.up2.release()
+        sums.down2.release()
+
+    def release():
+        for total in (sums.up, sums.down, sums.out, sums.query, sums.key, sums.value, sums.tail):
+            total.release()
 
     def out_grad():
         weight_grad(sums.out, mixs[...], lambda at: gatt[:, at])
@@ -972,11 +978,11 @@
     sums.value.step()
     pass_on(3)
     counts()
-    sums.down2.step()
     layer_out()
     sums.out.step()
     sums.up2.step()
     keys_of(0)
+    sums.down2.step()
     keys_of(1)
     sums.query.step()
     keys_of(2)
@@ -988,8 +994,9 @@
     sums.down2.step()
     first_back(1)
     pack_tail()
-    sums.up.step(2)
+    sums.up.step()
     sums.value.step()
+    sums.up.step()
     rows_back()
     layer_order()
     sums.tail.step()
@@ -1003,9 +1010,8 @@
     sums.up.step()
     sums.out.step()
     sums.query.step()
-    sums.value.step()
     sums.tail.step()
-    sums.value.step()
+    sums.value.step(2)
     sums.up.step()
     sums.key.step()
     sums.out.step()
@@ -1016,10 +1022,11 @@
     sums.up.step()
     sums.key.step()
     sums.out.step()
+    sums.value.step()
     sums.tail.step()
     sums.query.step()
-    sums.value.step()
     sums.down.step()
+    release()
     sums.key.step()
     drain()
     sums.value.step()
@@ -1089,9 +1096,10 @@
         def part(k):
             at = cut(k * at_once, at_once)
             ref.outb[i][at, :] = ref.inb[i][at, :].astype(F32)
+            pltpu.make_async_copy(ref.outb[i].at[at], targets[i].at[at], ref.osem.at[i]).start()
 
         loop(sources[i].shape[0] // at_once, part)
-        store(pltpu.make_async_copy(ref.outb[i], targets[i], ref.osem.at[i]))
+        stores.append(pltpu.make_async_copy(ref.outb[i], targets[i], ref.osem.at[i]))
 
     convert(0)
     convert(1)

time: 126 us -> 124 us (0.984)
  Pallas kernels: 124 us -> 121 us
    pallas_call x1, Pallas kernels: 116 us -> 113 us  [shards(): pl.pallas_call(functools.partial(kernel, (R, M, rows, D, F, S, near), nam...]
where the time goes in v4:
time: 124 us; the launch traced here: 122 us
  Pallas kernels  121 us (98%)
    pallas_call x1, Pallas kernels, shards(): pl.pallas_call(functools.partial(kernel, (R, M, rows, D, F, S, near), nam...  113 us
    pallas_call x1, Pallas kernels, shards(): pl.pallas_call(functools.partial(widen, (M, D, F, S), [*inputs, *finals,...  8.2 us

profile of v4, /device:TPU:0, one launch (start us, length us, event | category | flops | bytes accessed | tf_op | source)
XLA Modules:
  0.0 121.7 jit_solution(2782077270303617183)
XLA Ops:
  0.6 112.6 %layer.1 = (bf16[512,512]{1,0:T(8,128)(2,1)}, f32[512,512]{1,0:T(8,128)}, bf16[512,512]{1,0:T(8,128)(2,1)}, bf16[512,512]{1,0:T(8,128)(2,1)}, bf16[512,512]{1,0:...) custom-call(bf16[512,512]{1,0:T(8,128)(2,1)} %refs_0_.2, ...), custom_call_target="tpu_custom_call" | custom-call | tf_op jit(solution)/shard_map/layer/pallas_call | solution.py:1260
  113.3 8.2 %widen.1 = (bf16[512,512]{1,0:T(8,128)(2,1)}, f32[512,512]{1,0:T(8,128)}, f32[8,128]{1,0:T(8,128)}, f32[128,2048]{1,0:T(8,128)}, f32[2048]{0:T(1024)}, /*index=5...) custom-call(bf16[8,128]{1,0:T(8,128)(2,1)} %refs_0_.3, ...), custom_call_target="tpu_custom_call" | custom-call | tf_op jit(solution)/shard_map/widen/pallas_call | solution.py:1304

commit v5 on v4

--- a/solution.py
+++ b/solution.py
@@ -701,11 +701,11 @@
     def down_grad(total, count, which):
         ffn_grad(total, count, which, F, lambda p, f: actb[p, :, f], lambda p, at: cotb[:, at])
 
-    l_pass(0)
     up_grad(sums.up, 1, lambda u: y)
     down_grad(sums.down, 1, lambda u: y)
     sums.up.step()
     sums.down.step()
+    l_pass(0)
 
     def feed_other(t):
         @pl.when(t == 0)

time: 124 us -> 123 us (level)
  no operation moved by 1% of the time
where the time goes in v5:
time: 123 us; the launch traced here: 122 us
  Pallas kernels  121 us (98%)
    pallas_call x1, Pallas kernels, shards(): pl.pallas_call(functools.partial(kernel, (R, M, rows, D, F, S, near), nam...  113 us
    pallas_call x1, Pallas kernels, shards(): pl.pallas_call(functools.partial(widen, (M, D, F, S), [*inputs, *finals,...  8.2 us

profile of v5, /device:TPU:0, one launch (start us, length us, event | category | flops | bytes accessed | tf_op | source)
XLA Modules:
  0.0 121.9 jit_solution(3574374345005784183)
XLA Ops:
  0.6 112.8 %layer.1 = (bf16[512,512]{1,0:T(8,128)(2,1)}, f32[512,512]{1,0:T(8,128)}, bf16[512,512]{1,0:T(8,128)(2,1)}, bf16[512,512]{1,0:T(8,128)(2,1)}, bf16[512,512]{1,0:...) custom-call(bf16[512,512]{1,0:T(8,128)(2,1)} %refs_0_.2, ...), custom_call_target="tpu_custom_call" | custom-call | tf_op jit(solution)/shard_map/layer/pallas_call | solution.py:1260
  113.5 8.2 %widen.1 = (bf16[512,512]{1,0:T(8,128)(2,1)}, f32[512,512]{1,0:T(8,128)}, f32[8,128]{1,0:T(8,128)}, f32[128,2048]{1,0:T(8,128)}, f32[2048]{0:T(1024)}, /*index=5...) custom-call(bf16[8,128]{1,0:T(8,128)(2,1)} %refs_0_.3, ...), custom_call_target="tpu_custom_call" | custom-call | tf_op jit(solution)/shard_map/widen/pallas_call | solution.py:1304
